TPU v7x, 128 devices: a whole 4x4x4 slice. The times are simulated.
128 devices in a mesh: sec: 16 (over x, y), strip: 8 (over z, core).
Axes of the slice: x: 4, y: 4, z: 4, core: 2. Of those that a mesh axis runs over, the one named last changes fastest.
Arguments:
- start_offsets: float32 [2, 16, 768, 2048], P(None, 'sec', 'strip'), may hold values from -0.4 to 0.4
- section_flow: float32 [2, 16, 768, 2048], P(None, 'sec', 'strip'), may hold values from -1.5 to 1.5, as said below
- fixed_nodes: int32 [16, 768, 2048], P('sec', 'strip'), may hold values 0 or 1
- links_across: int32 [16, 768, 2048], P('sec', 'strip'), may hold values 0 or 1
- links_down: int32 [16, 768, 2048], P('sec', 'strip'), may hold values 0 or 1
Outputs:
- final_offsets: float32 [2, 16, 768, 2048], P(None, 'sec', 'strip')
- final_speeds: float32 [2, 16, 768, 2048], P(None, 'sec', 'strip')
Inputs may be any that keep to these rules, and one draw needn't show every extreme that they name: `section_flow`: entries of section 0 take part in no spring.
All inputs are finite; a program needn't handle non-finite values. No bound on the sum of `fixed_nodes` or of `links_across` or of `links_down` on one device may be relied on, other than what follows from the above.
Results may differ from a plain program's by a relative error of at most 0.00017.
Values sent between devices are 32-bit elements; how exact they have to be, the bound alone decides.
A program may use at most 64 MiB of HBM per device.

v0:
```python
import jax
import jax.numpy as jnp
from jax import lax
from jax.sharding import Mesh
from jax.sharding import PartitionSpec as P

SWEEPS = 2
ROUNDS = 2
SUBSTEPS = 4
SEC = ("sec_0", "sec_1")
STRIP = ("strip_0", "strip_1")


SPRING = 1.0
COUPLING = 0.5
STEP_SIZE = 0.4
DAMPING = 0.9
SPEED_CAP = 0.05
EPSILON = 1e-06


def extended(x, sides, width):
    for axis, dim in sides:
        peers, length = (lax.axis_size(axis), x.shape[dim])
        up = [(i, (i + 1) % peers) for i in range(peers - 1)]
        down = [(j, i) for i, j in up]
        last = lax.slice_in_dim(x, length - width, length, axis=dim)
        first = lax.slice_in_dim(x, 0, width, axis=dim)
        before = lax.ppermute(last, axis, up)
        after = lax.ppermute(first, axis, down)
        x = jnp.concatenate([before, x, after], axis=dim)
    return x


def shifted(x, axis, by):
    peers = lax.axis_size(axis)
    pairs = [(i, i + by) for i in range(peers) if 0 <= i + by < peers]
    return lax.ppermute(x, axis, pairs)


def from_everyone(x, axis):
    copies = jnp.broadcast_to(x, (lax.axis_size(axis), *x.shape))
    return lax.all_to_all(copies, axis, split_axis=0, concat_axis=0, tiled=True)


def over_copies(x, axis):
    return from_everyone(x, axis).sum(axis=0)


def one_axis_at_a_time(x, axes):
    far, near = axes
    return over_copies(over_copies(x, near), far)


def along_cols(values, lower, upper):
    widths = [(0, 0)] * (values.ndim - 1) + [(lower, upper)]
    return jnp.pad(values, widths)


def along_rows(values, lower, upper):
    widths = [(0, 0)] * (values.ndim - 2) + [(lower, upper), (0, 0)]
    return jnp.pad(values, widths)


def spring_forces(offsets, across, down):
    across_x = offsets[0, ..., 1:] - offsets[0, ..., :-1] + 1.0
    across_y = offsets[1, ..., 1:] - offsets[1, ..., :-1]
    tension = 0.5 * SPRING * (across_x * across_x + across_y * across_y - 1.0) * across[..., :-1]
    force_x = along_cols(tension * across_x, 0, 1) - along_cols(tension * across_x, 1, 0)
    force_y = along_cols(tension * across_y, 0, 1) - along_cols(tension * across_y, 1, 0)
    down_x = offsets[0, ..., 1:, :] - offsets[0, ..., :-1, :]
    down_y = offsets[1, ..., 1:, :] - offsets[1, ..., :-1, :] + 1.0
    strain = 0.5 * SPRING * (down_x * down_x + down_y * down_y - 1.0) * down[..., :-1, :]
    force_x = force_x + along_rows(strain * down_x, 0, 1) - along_rows(strain * down_x, 1, 0)
    force_y = force_y + along_rows(strain * down_y, 0, 1) - along_rows(strain * down_y, 1, 0)
    return jnp.stack([force_x, force_y])


def advance(offsets, speeds, across, down, mobility, target, section_links):
    force = spring_forces(offsets, across, down) + COUPLING * (target - section_links * offsets)
    speeds = mobility * (DAMPING * speeds + STEP_SIZE * force)
    return (offsets + STEP_SIZE * speeds, speeds)


def on_device(start_offsets, section_flow, fixed_nodes, links_across, links_down):
    sections_here, rows_here, columns = fixed_nodes.shape
    total_sections = sections_here * lax.axis_size(SEC)
    total_rows = rows_here * lax.axis_size(STRIP)
    entries = 2.0 * total_sections * total_rows * columns
    section_index = lax.axis_index(SEC) * sections_here + jnp.arange(sections_here)
    has_below = (section_index > 0).astype(jnp.float32)[:, None, None]
    has_above = (section_index < total_sections - 1).astype(jnp.float32)[:, None, None]
    section_links = has_below + has_above
    column_index = jnp.arange(columns)
    row_index = lax.axis_index(STRIP) * rows_here + jnp.arange(rows_here)
    across = links_across.astype(jnp.float32) * (column_index < columns - 1).astype(jnp.float32)
    down = (
        links_down.astype(jnp.float32) * (row_index < total_rows - 1).astype(jnp.float32)[:, None]
    )
    mobility = 1.0 - fixed_nodes.astype(jnp.float32)
    coefficients = extended(jnp.stack([mobility, across, down]), ((STRIP, 2),), SUBSTEPS)
    offsets = start_offsets
    speeds = jnp.zeros_like(start_offsets)
    for sweep_id in range(SWEEPS):
        lower = shifted(offsets[:, -1], SEC, 1)
        upper = shifted(offsets[:, 0] - section_flow[:, 0], SEC, -1)
        below = jnp.concatenate([lower[:, None], offsets[:, :-1]], axis=1) + section_flow
        above = jnp.concatenate([offsets[:, 1:] - section_flow[:, 1:], upper[:, None]], axis=1)
        target = has_below * below + has_above * above
        target_wide = extended(target, ((STRIP, 2),), SUBSTEPS)
        for round_id in range(ROUNDS):
            power = one_axis_at_a_time(
                jnp.sum(speeds * speeds), (("sec_0", "sec_1", "strip_0"), "strip_1")
            )
            spread = jnp.sqrt(power / entries + EPSILON)
            speeds = speeds * jnp.minimum(1.0, SPEED_CAP / spread)
            state = extended(jnp.stack([offsets, speeds]), ((STRIP, 3),), SUBSTEPS)
            offsets_wide = state[0]
            speeds_wide = state[1]
            for substep_id in range(SUBSTEPS):
                offsets_wide, speeds_wide = advance(
                    offsets_wide,
                    speeds_wide,
                    coefficients[1],
                    coefficients[2],
                    coefficients[0],
                    target_wide,
                    section_links,
                )
            offsets = offsets_wide[:, :, SUBSTEPS : SUBSTEPS + rows_here]
            speeds = speeds_wide[:, :, SUBSTEPS : SUBSTEPS + rows_here]
    return (offsets, speeds)


def solution(mesh):
    finer = Mesh(mesh.devices.reshape(4, 4, 4, 2), ("sec_0", "sec_1", "strip_0", "strip_1"))
    return jax.shard_map(
        on_device,
        mesh=finer,
        in_specs=(
            P(None, SEC, STRIP, None),
            P(None, SEC, STRIP, None),
            P(SEC, STRIP, None),
            P(SEC, STRIP, None),
            P(SEC, STRIP, None),
        ),
        out_specs=(P(None, SEC, STRIP, None), P(None, SEC, STRIP, None)),
        check_vma=False,
    )
```

profile of v0, /device:TPU:1, one launch (start us, length us, event | category | flops | bytes accessed | tf_op | source)
XLA Modules:
  0.0 285.3 jit_solution(10401596198012690068)
XLA Ops:
  0.6 1.8 pad_slice_fusion.1
  2.4 4.9 %collective-permute-start = (f32[2,2,1,4,2048]{4,3,1,2,0:T(4,128)}, f32[2,2,1,4,2048]{4,3,1,2,0:T(4,128)}, u32[]{:S(2)}, u32[]{:S(2)}) collective-permute-start(f32[2,2,1,4,2048]{4,3,1,2,0:T(4,128)} %get-tuple-element.99), channel_id=1, source_target_pairs={{0,1},{1,2},{2,3},{3,4},{4,5},{5,6},{6,7},{8,9},{9,10},{10,11},{11... | collective-permute-start | bytes 393224 | tf_op jit(solution)/shard_map/ppermute | solution.py:29
  7.3 1.9 collective-permute-start.1
  9.4 1.3 multiply_bitcast_fusion.3
  11.6 3.6 %collective-permute-start.2 = (f32[3,1,4,2048]{3,2,1,0:T(4,128)S(1)}, f32[3,1,4,2048]{3,2,1,0:T(4,128)}, u32[]{:S(2)}, u32[]{:S(2)}) collective-permute-start(f32[3,1,4,2048]{3,2,1,0:T(4,128)S(1)} %get-tuple-element.91), channel_id=1, source_target_pairs={{0,1},{1,2},{2,3},{3,4},{4,5},{5,6},{6,7},{8,9},{9,10},{10,11},{11... | collective-permute-start | bytes 294920 | tf_op jit(solution)/shard_map/ppermute | solution.py:29
  15.3 1.9 collective-permute-start.3
  17.2 2.8 bitcast_subtract_fusion.1
  20.0 1.3 collective-permute-start.5
  21.3 1.4 broadcast_bitcast_fusion
  22.7 3.5 %stack.191 = f32[2,2,1,96,2048]{4,3,1,2,0:T(8,128)} pad(f32[1,2,1,96,2048]{4,3,1,2,0:T(8,128)} %bitcast, f32[]{:T(128)} %constant.85.clone.1), padding=0_1x0_0x0_0x0_0x0_0 | pad | bytes 4718596 | tf_op jit(solution)/shard_map/stack | solution.py:117
  26.2 4.1 %collective-permute-start.4 = (f32[2,96,2048]{2,1,0:T(8,128)}, f32[2,96,2048]{2,1,0:T(8,128)S(1)}, u32[]{:S(2)}, u32[]{:S(2)}) collective-permute-start(f32[2,96,2048]{2,1,0:T(8,128)} %bitcast.20), channel_id=1, source_target_pairs={{0,8},{8,16},{16,24},{24,32},{32,40},{40,48},{48,56},{56,64},{64,7... | collective-permute-start | bytes 4718600 | tf_op jit(solution)/shard_map/ppermute | solution.py:38
  30.3 1.3 pad_maximum_fusion.4
  31.7 1.7 copy-done.16
  33.4 1.4 pad_maximum_fusion
  36.5 21.0 %collective-permute-done.5 = f32[2,96,2048]{2,1,0:T(8,128)} collective-permute-done((f32[2,96,2048]{2,1,0:T(8,128)}, f32[2,96,2048]{2,1,0:T(8,128)}, u32[]{:S(2)}, u32[]{:S(2)}) %collective-permute-start.5) | collective-permute-done | bytes 1572896 | tf_op jit(solution)/shard_map/ppermute | solution.py:38
  57.5 6.6 %collective-permute-done.4 = f32[2,96,2048]{2,1,0:T(8,128)S(1)} collective-permute-done((f32[2,96,2048]{2,1,0:T(8,128)}, f32[2,96,2048]{2,1,0:T(8,128)S(1)}, u32[]{:S(2)}, u32[]{:S(2)}) %collective-permute-start.4) | collective-permute-done | bytes 1572896 | tf_op jit(solution)/shard_map/ppermute | solution.py:38
  64.2 1.8 bitcast_add_fusion.2
  66.0 4.3 %collective-permute-start.6 = (f32[2,1,4,2048]{3,2,0,1:T(4,128)S(1)}, f32[2,1,4,2048]{3,2,0,1:T(4,128)S(1)}, u32[]{:S(2)}, u32[]{:S(2)}) collective-permute-start(f32[2,1,4,2048]{3,2,0,1:T(4,128)S(1)} %get-tuple-element.97), channel_id=1, source_target_pairs={{0,1},{1,2},{2,3},{3,4},{4,5},{5,6},{6,7},{8,9},{9,10},{10,11},{11... | collective-permute-start | bytes 196616 | tf_op jit(solution)/shard_map/ppermute | solution.py:29
  70.3 2.1 collective-permute-start.7
  72.8 3.2 %collective-permute-done.7 = f32[2,1,4,2048]{3,2,0,1:T(4,128)S(1)} collective-permute-done((f32[2,1,4,2048]{3,2,0,1:T(4,128)S(1)}, f32[2,1,4,2048]{3,2,0,1:T(4,128)S(1)}, u32[]{:S(2)}, u32[]{:S(2)}) %collective-permute-start.7) | collective-permute-done | bytes 65568 | tf_op jit(solution)/shard_map/ppermute | solution.py:30
  78.4 1.4 fusion.31
  84.0 1.4 bitcast_multiply_fusion.23
  85.4 2.4 fusion.64
  88.4 3.4 %all_to_all.40 = f32[2,1,1]{2,1,0:T(1,128)S(1)} all-to-all(f32[2,1,1]{2,1,0:T(1,128)S(1)} %broadcast_in_dim.17), channel_id=1, replica_groups=mesh['sec_0'=4,'sec_1'=4,'strip_0'=4,'strip_1'=2] {'strip_1'}, dimensions={0} | all-to-all | bytes 16 | tf_op jit(solution)/shard_map/all_to_all | solution.py:43
  92.9 20.8 %all_to_all.41 = f32[64,1,1]{2,1,0:T(1,128)S(1)} all-to-all(f32[64,1,1]{2,1,0:T(1,128)S(1)} %broadcast_in_dim.18), channel_id=1, replica_groups=mesh['sec_0'=4,'sec_1'=4,'strip_0'=4,'strip_1'=2] {'sec_0','sec_1','stri..., dimensions={0} | all-to-all | bytes 512 | tf_op jit(solution)/shard_map/all_to_all | solution.py:43
  115.1 1.8 multiply_bitcast_fusion.2
  117.1 3.9 %collective-permute-start.8 = (f32[2,2,1,4,2048]{4,3,1,2,0:T(4,128)S(1)}, f32[2,2,1,4,2048]{4,3,1,2,0:T(4,128)S(1)}, u32[]{:S(2)}, u32[]{:S(2)}) collective-permute-start(f32[2,2,1,4,2048]{4,3,1,2,0:T(4,128)S(1)} %get-tuple-element.36), channel_id=1, source_target_pairs={{0,1},{1,2},{2,3},{3,4},{4,5},{5,6},{6,7},{8,9},{9,10},{10,11},{11... | collective-permute-start | bytes 393224 | tf_op jit(solution)/shard_map/ppermute | solution.py:29
  120.9 2.3 collective-permute-start.9
  123.3 3.9 %collective-permute-done.9 = f32[2,2,1,4,2048]{4,3,1,2,0:T(4,128)S(1)} collective-permute-done((f32[2,2,1,4,2048]{4,3,1,2,0:T(4,128)S(1)}, f32[2,2,1,4,2048]{4,3,1,2,0:T(4,128)S(1)}, u32[]{:S(2)}, u32[]{:S(2)}) %collective-permute-start.9) | collective-permute-done | bytes 131104 | tf_op jit(solution)/shard_map/ppermute | solution.py:30
  129.6 1.1 copy-done.3
  130.7 1.1 fusion.34
  135.9 1.4 fusion.36
  138.9 1.7 bitcast_multiply_fusion.19
  140.6 1.2 copy-done.11
  143.5 3.4 %all_to_all.42 = f32[2,1,1]{2,1,0:T(1,128)S(1)} all-to-all(f32[2,1,1]{2,1,0:T(1,128)S(1)} %broadcast_in_dim.19), channel_id=1, replica_groups=mesh['sec_0'=4,'sec_1'=4,'strip_0'=4,'strip_1'=2] {'strip_1'}, dimensions={0} | all-to-all | bytes 16 | tf_op jit(solution)/shard_map/all_to_all | solution.py:43
  147.5 1.3 broadcast_in_dim.20
  148.7 5.5 %all-to-all-start.3 = ((f32[64,1,1]{2,1,0:T(1,128)}), f32[64,1,1]{2,1,0:T(1,128)S(1)}, u32[]{:S(2)}, u32[]{:S(2)}) async-start(f32[64,1,1]{2,1,0:T(1,128)} %broadcast_in_dim.20), calls=%async_computation.3 | async-start | bytes 65536 | tf_op jit(solution)/shard_map/all_to_all | solution.py:43
  154.3 5.6 %bitcast_subtract_fusion = (f32[2,96,2048]{2,1,0:T(8,128)}, f32[2,1,96,2048]{3,2,0,1:T(8,128)}) fusion(f32[2,1,96,2048]{3,2,1,0:T(8,128)} %param.6, f32[2,1,104,2048]{3,2,0,1:T(8,128)} %broadcast_bitcast_fusion, f32[2,1,104,2048]{3,2,0,1:T(8,128)} %copy-done.11, f32[2,1,104,2048]{3,2,0,1:T(8,128)} %copy-done.5), kind=kLoop, calls=%fused_computation.164 | loop fusion | flops 1179648 | bytes 9437184 | tf_op jit(solution)/shard_map/sub | solution.py:106
  159.9 2.9 %all-to-all-done.3 = f32[64,1,1]{2,1,0:T(1,128)S(1)} async-done(((f32[64,1,1]{2,1,0:T(1,128)}), f32[64,1,1]{2,1,0:T(1,128)S(1)}, u32[]{:S(2)}, u32[]{:S(2)}) %all-to-all-start.3) | async-done | bytes 288 | tf_op jit(solution)/shard_map/all_to_all | solution.py:43
  164.1 1.8 multiply_bitcast_fusion.1
  166.0 4.0 %collective-permute-start.10 = (f32[2,2,1,4,2048]{4,3,1,2,0:T(4,128)S(1)}, f32[2,2,1,4,2048]{4,3,1,2,0:T(4,128)S(1)}, u32[]{:S(2)}, u32[]{:S(2)}) collective-permute-start(f32[2,2,1,4,2048]{4,3,1,2,0:T(4,128)S(1)} %get-tuple-element.34), channel_id=1, source_target_pairs={{0,1},{1,2},{2,3},{3,4},{4,5},{5,6},{6,7},{8,9},{9,10},{10,11},{11... | collective-permute-start | bytes 393224 | tf_op jit(solution)/shard_map/ppermute | solution.py:29
  170.0 1.9 collective-permute-start.11
  172.0 2.3 collective-permute-start.12
  174.3 1.3 collective-permute-start.13
  178.3 29.1 %collective-permute-done.12 = f32[2,96,2048]{2,1,0:T(8,128)S(1)} collective-permute-done((f32[2,96,2048]{2,1,0:T(8,128)S(1)}, f32[2,96,2048]{2,1,0:T(8,128)S(1)}, u32[]{:S(2)}, u32[]{:S(2)}) %collective-permute-start.12) | collective-permute-done | bytes 1572896 | tf_op jit(solution)/shard_map/ppermute | solution.py:38
  207.5 4.2 %collective-permute-done.13 = f32[2,96,2048]{2,1,0:T(8,128)S(1)} collective-permute-done((f32[2,96,2048]{2,1,0:T(8,128)S(1)}, f32[2,96,2048]{2,1,0:T(8,128)S(1)}, u32[]{:S(2)}, u32[]{:S(2)}) %collective-permute-start.13) | collective-permute-done | bytes 1572896 | tf_op jit(solution)/shard_map/ppermute | solution.py:38
  212.2 3.3 %collective-permute-start.14 = (f32[2,1,4,2048]{3,2,0,1:T(4,128)S(1)}, f32[2,1,4,2048]{3,2,0,1:T(4,128)S(1)}, u32[]{:S(2)}, u32[]{:S(2)}) collective-permute-start(f32[2,1,4,2048]{3,2,0,1:T(4,128)S(1)} %get-tuple-element.95), channel_id=1, source_target_pairs={{0,1},{1,2},{2,3},{3,4},{4,5},{5,6},{6,7},{8,9},{9,10},{10,11},{11... | collective-permute-start | bytes 196616 | tf_op jit(solution)/shard_map/ppermute | solution.py:29
  215.5 1.9 collective-permute-start.15
  217.7 3.3 %collective-permute-done.15 = f32[2,1,4,2048]{3,2,0,1:T(4,128)S(1)} collective-permute-done((f32[2,1,4,2048]{3,2,0,1:T(4,128)S(1)}, f32[2,1,4,2048]{3,2,0,1:T(4,128)S(1)}, u32[]{:S(2)}, u32[]{:S(2)}) %collective-permute-start.15) | collective-permute-done | bytes 65568 | tf_op jit(solution)/shard_map/ppermute | solution.py:30
  223.6 1.4 fusion.61
  229.2 1.4 fusion.28
  230.7 1.2 copy-done.9
  233.6 3.4 %all_to_all.43 = f32[2,1,1]{2,1,0:T(1,128)S(1)} all-to-all(f32[2,1,1]{2,1,0:T(1,128)S(1)} %broadcast_in_dim.22), channel_id=1, replica_groups=mesh['sec_0'=4,'sec_1'=4,'strip_0'=4,'strip_1'=2] {'strip_1'}, dimensions={0} | all-to-all | bytes 16 | tf_op jit(solution)/shard_map/all_to_all | solution.py:43
  237.5 1.3 broadcast_in_dim.23
  238.8 9.5 %all-to-all-start.5 = ((f32[64,1,1]{2,1,0:T(1,128)}), f32[64,1,1]{2,1,0:T(1,128)S(1)}, u32[]{:S(2)}, u32[]{:S(2)}) async-start(f32[64,1,1]{2,1,0:T(1,128)} %broadcast_in_dim.23), calls=%async_computation.5 | async-start | bytes 65536 | tf_op jit(solution)/shard_map/all_to_all | solution.py:43
  248.3 4.2 %fusion.63 = f32[1,2,1,96,2048]{4,3,1,2,0:T(8,128)} fusion(f32[2,1,104,2048]{3,2,0,1:T(8,128)} %copy-done.4, f32[2,1,104,2048]{3,2,0,1:T(8,128)} %bitcast.1107, f32[2,1,104,2048]{3,2,0,1:T(8,128)} %broadcast_bitcast_fusion), kind=kLoop, calls=%fused_computation.155 | loop fusion | flops 786432 | bytes 6291456 | tf_op jit(solution)/shard_map/stack | solution.py:117
  252.6 4.1 %all-to-all-done.5 = f32[64,1,1]{2,1,0:T(1,128)S(1)} async-done(((f32[64,1,1]{2,1,0:T(1,128)}), f32[64,1,1]{2,1,0:T(1,128)S(1)}, u32[]{:S(2)}, u32[]{:S(2)}) %all-to-all-start.5) | async-done | bytes 288 | tf_op jit(solution)/shard_map/all_to_all | solution.py:43
  258.0 1.8 multiply_bitcast_fusion
  260.0 3.9 %collective-permute-start.16 = (f32[2,2,1,4,2048]{4,3,1,2,0:T(4,128)S(1)}, f32[2,2,1,4,2048]{4,3,1,2,0:T(4,128)S(1)}, u32[]{:S(2)}, u32[]{:S(2)}) collective-permute-start(f32[2,2,1,4,2048]{4,3,1,2,0:T(4,128)S(1)} %get-tuple-element.32), channel_id=1, source_target_pairs={{0,1},{1,2},{2,3},{3,4},{4,5},{5,6},{6,7},{8,9},{9,10},{10,11},{11... | collective-permute-start | bytes 393224 | tf_op jit(solution)/shard_map/ppermute | solution.py:29
  263.9 2.1 collective-permute-start.17
  266.0 4.1 %collective-permute-done.17 = f32[2,2,1,4,2048]{4,3,1,2,0:T(4,128)S(1)} collective-permute-done((f32[2,2,1,4,2048]{4,3,1,2,0:T(4,128)S(1)}, f32[2,2,1,4,2048]{4,3,1,2,0:T(4,128)S(1)}, u32[]{:S(2)}, u32[]{:S(2)}) %collective-permute-start.17) | collective-permute-done | bytes 131104 | tf_op jit(solution)/shard_map/ppermute | solution.py:30
  276.0 1.4 multiply_add_fusion.1
  281.5 1.4 fusion.60
  282.9 2.1 slice_add_fusion
  (151 shorter events, 46.2 us)
Async XLA Ops:
  0.6 8.7 %copy-start.20 = (s32[1,96,2048]{2,1,0:T(8,128)S(1)}, s32[1,96,2048]{2,1,0:T(8,128)}, u32[]{:S(2)}) copy-start(s32[1,96,2048]{2,1,0:T(8,128)} %param.7) | copy-start | bytes 2359300
  0.6 8.8 %copy-start.21 = (s32[1,96,2048]{2,1,0:T(8,128)S(1)}, s32[1,96,2048]{2,1,0:T(8,128)}, u32[]{:S(2)}) copy-start(s32[1,96,2048]{2,1,0:T(8,128)} %param.9) | copy-start | bytes 2359300
  2.4 29.3 %collective-permute-start = (f32[2,2,1,4,2048]{4,3,1,2,0:T(4,128)}, f32[2,2,1,4,2048]{4,3,1,2,0:T(4,128)}, u32[]{:S(2)}, u32[]{:S(2)}) collective-permute-start(f32[2,2,1,4,2048]{4,3,1,2,0:T(4,128)} %get-tuple-element.99), channel_id=1, source_target_pairs={{0,1},{1,2},{2,3},{3,4},{4,5},{5,6},{6,7},{8,9},{9,10},{10,11},{11... | collective-permute-start | bytes 393224 | tf_op jit(solution)/shard_map/ppermute | solution.py:29
  7.3 24.4 %collective-permute-start.1 = (f32[2,2,1,4,2048]{4,3,1,2,0:T(4,128)S(1)}, f32[2,2,1,4,2048]{4,3,1,2,0:T(4,128)}, u32[]{:S(2)}, u32[]{:S(2)}) collective-permute-start(f32[2,2,1,4,2048]{4,3,1,2,0:T(4,128)S(1)} %get-tuple-element.100), channel_id=1, source_target_pairs={{1,0},{2,1},{3,2},{4,3},{5,4},{6,5},{7,6},{9,8},{10,9},{11,10},{12... | collective-permute-start | bytes 393224 | tf_op jit(solution)/shard_map/ppermute | solution.py:30
  10.7 0.9 copy-start.17
  10.7 6.5 %copy-start.6 = (f32[2,1,96,2048]{3,2,1,0:T(8,128)S(1)}, f32[2,1,96,2048]{3,2,1,0:T(8,128)}, u32[]{:S(2)}) copy-start(f32[2,1,96,2048]{3,2,1,0:T(8,128)} %param.6) | copy-start | bytes 4718596
  11.6 14.5 %collective-permute-start.2 = (f32[3,1,4,2048]{3,2,1,0:T(4,128)S(1)}, f32[3,1,4,2048]{3,2,1,0:T(4,128)}, u32[]{:S(2)}, u32[]{:S(2)}) collective-permute-start(f32[3,1,4,2048]{3,2,1,0:T(4,128)S(1)} %get-tuple-element.91), channel_id=1, source_target_pairs={{0,1},{1,2},{2,3},{3,4},{4,5},{5,6},{6,7},{8,9},{9,10},{10,11},{11... | collective-permute-start | bytes 294920 | tf_op jit(solution)/shard_map/ppermute | solution.py:29
  15.3 15.0 %collective-permute-start.3 = (f32[3,1,4,2048]{3,2,1,0:T(4,128)S(1)}, f32[3,1,4,2048]{3,2,1,0:T(4,128)}, u32[]{:S(2)}, u32[]{:S(2)}) collective-permute-start(f32[3,1,4,2048]{3,2,1,0:T(4,128)S(1)} %get-tuple-element.92), channel_id=1, source_target_pairs={{1,0},{2,1},{3,2},{4,3},{5,4},{6,5},{7,6},{9,8},{10,9},{11,10},{12... | collective-permute-start | bytes 294920 | tf_op jit(solution)/shard_map/ppermute | solution.py:30
  20.0 37.6 %collective-permute-start.5 = (f32[2,96,2048]{2,1,0:T(8,128)}, f32[2,96,2048]{2,1,0:T(8,128)}, u32[]{:S(2)}, u32[]{:S(2)}) collective-permute-start(f32[2,96,2048]{2,1,0:T(8,128)} %bitcast_subtract_fusion.1), channel_id=1, source_target_pairs={{8,0},{16,8},{24,16},{32,24},{40,32},{48,40},{56,48},{64,56},{72,6... | collective-permute-start | bytes 4718600 | tf_op jit(solution)/shard_map/ppermute | solution.py:38
  22.7 7.6 %copy-start.18 = (f32[1,1,96,2048]{3,2,1,0:T(8,128)S(1)}, f32[1,1,96,2048]{3,2,1,0:T(8,128)}, u32[]{:S(2)}) copy-start(f32[1,1,96,2048]{3,2,1,0:T(8,128)} %copy-done.17) | copy-start | bytes 2359300
  26.2 38.0 %collective-permute-start.4 = (f32[2,96,2048]{2,1,0:T(8,128)}, f32[2,96,2048]{2,1,0:T(8,128)S(1)}, u32[]{:S(2)}, u32[]{:S(2)}) collective-permute-start(f32[2,96,2048]{2,1,0:T(8,128)} %bitcast.20), channel_id=1, source_target_pairs={{0,8},{8,16},{16,24},{24,32},{32,40},{40,48},{48,56},{56,64},{64,7... | collective-permute-start | bytes 4718600 | tf_op jit(solution)/shard_map/ppermute | solution.py:38
  31.5 1.9 copy-start.16
  36.2 28.0 %copy-start.7 = (f32[2,1,96,2048]{3,2,1,0:T(8,128)S(1)}, f32[2,1,96,2048]{3,2,1,0:T(8,128)}, u32[]{:S(2)}) copy-start(f32[2,1,96,2048]{3,2,1,0:T(8,128)} %param.6) | copy-start | bytes 4718596
  66.0 18.0 %copy-start.2 = (f32[2,1,96,2048]{3,2,0,1:T(8,128)}, f32[2,1,96,2048]{3,2,0,1:T(8,128)S(1)}, u32[]{:S(2)}) copy-start(f32[2,1,96,2048]{3,2,0,1:T(8,128)S(1)} %bitcast_add_fusion.2) | copy-start | bytes 4718596
  66.0 6.7 %collective-permute-start.6 = (f32[2,1,4,2048]{3,2,0,1:T(4,128)S(1)}, f32[2,1,4,2048]{3,2,0,1:T(4,128)S(1)}, u32[]{:S(2)}, u32[]{:S(2)}) collective-permute-start(f32[2,1,4,2048]{3,2,0,1:T(4,128)S(1)} %get-tuple-element.97), channel_id=1, source_target_pairs={{0,1},{1,2},{2,3},{3,4},{4,5},{5,6},{6,7},{8,9},{9,10},{10,11},{11... | collective-permute-start | bytes 196616 | tf_op jit(solution)/shard_map/ppermute | solution.py:29
  70.3 5.6 %collective-permute-start.7 = (f32[2,1,4,2048]{3,2,0,1:T(4,128)S(1)}, f32[2,1,4,2048]{3,2,0,1:T(4,128)S(1)}, u32[]{:S(2)}, u32[]{:S(2)}) collective-permute-start(f32[2,1,4,2048]{3,2,0,1:T(4,128)S(1)} %get-tuple-element.98), channel_id=1, source_target_pairs={{1,0},{2,1},{3,2},{4,3},{5,4},{6,5},{7,6},{9,8},{10,9},{11,10},{12... | collective-permute-start | bytes 196616 | tf_op jit(solution)/shard_map/ppermute | solution.py:30
  83.9 1.5 copy-start.10
  85.4 2.4 copy-start.15
  115.1 1.9 copy-start.13
  117.1 6.2 %collective-permute-start.8 = (f32[2,2,1,4,2048]{4,3,1,2,0:T(4,128)S(1)}, f32[2,2,1,4,2048]{4,3,1,2,0:T(4,128)S(1)}, u32[]{:S(2)}, u32[]{:S(2)}) collective-permute-start(f32[2,2,1,4,2048]{4,3,1,2,0:T(4,128)S(1)} %get-tuple-element.36), channel_id=1, source_target_pairs={{0,1},{1,2},{2,3},{3,4},{4,5},{5,6},{6,7},{8,9},{9,10},{10,11},{11... | collective-permute-start | bytes 393224 | tf_op jit(solution)/shard_map/ppermute | solution.py:29
  120.9 6.3 %collective-permute-start.9 = (f32[2,2,1,4,2048]{4,3,1,2,0:T(4,128)S(1)}, f32[2,2,1,4,2048]{4,3,1,2,0:T(4,128)S(1)}, u32[]{:S(2)}, u32[]{:S(2)}) collective-permute-start(f32[2,2,1,4,2048]{4,3,1,2,0:T(4,128)S(1)} %get-tuple-element.37), channel_id=1, source_target_pairs={{1,0},{2,1},{3,2},{4,3},{5,4},{6,5},{7,6},{9,8},{10,9},{11,10},{12... | collective-permute-start | bytes 393224 | tf_op jit(solution)/shard_map/ppermute | solution.py:30
  129.3 1.4 copy-start.3
  137.3 1.6 copy-start.5
  140.6 1.2 copy-start.11
  148.7 14.0 %all-to-all-start.3 = ((f32[64,1,1]{2,1,0:T(1,128)}), f32[64,1,1]{2,1,0:T(1,128)S(1)}, u32[]{:S(2)}, u32[]{:S(2)}) async-start(f32[64,1,1]{2,1,0:T(1,128)} %broadcast_in_dim.20), calls=%async_computation.3 | async-start | bytes 65536 | tf_op jit(solution)/shard_map/all_to_all | solution.py:43
  164.0 1.9 copy-start.12
  166.0 8.3 %copy-start.19 = (f32[2,96,2048]{2,1,0:T(8,128)S(1)}, f32[2,96,2048]{2,1,0:T(8,128)}, u32[]{:S(2)}) copy-start(f32[2,96,2048]{2,1,0:T(8,128)} %get-tuple-element.8) | copy-start | bytes 4718596
  166.0 9.6 %collective-permute-start.10 = (f32[2,2,1,4,2048]{4,3,1,2,0:T(4,128)S(1)}, f32[2,2,1,4,2048]{4,3,1,2,0:T(4,128)S(1)}, u32[]{:S(2)}, u32[]{:S(2)}) collective-permute-start(f32[2,2,1,4,2048]{4,3,1,2,0:T(4,128)S(1)} %get-tuple-element.34), channel_id=1, source_target_pairs={{0,1},{1,2},{2,3},{3,4},{4,5},{5,6},{6,7},{8,9},{9,10},{10,11},{11... | collective-permute-start | bytes 393224 | tf_op jit(solution)/shard_map/ppermute | solution.py:29
  170.0 6.3 %collective-permute-start.11 = (f32[2,2,1,4,2048]{4,3,1,2,0:T(4,128)S(1)}, f32[2,2,1,4,2048]{4,3,1,2,0:T(4,128)S(1)}, u32[]{:S(2)}, u32[]{:S(2)}) collective-permute-start(f32[2,2,1,4,2048]{4,3,1,2,0:T(4,128)S(1)} %get-tuple-element.35), channel_id=1, source_target_pairs={{1,0},{2,1},{3,2},{4,3},{5,4},{6,5},{7,6},{9,8},{10,9},{11,10},{12... | collective-permute-start | bytes 393224 | tf_op jit(solution)/shard_map/ppermute | solution.py:30
  172.0 35.5 %collective-permute-start.12 = (f32[2,96,2048]{2,1,0:T(8,128)S(1)}, f32[2,96,2048]{2,1,0:T(8,128)S(1)}, u32[]{:S(2)}, u32[]{:S(2)}) collective-permute-start(f32[2,96,2048]{2,1,0:T(8,128)S(1)} %bitcast.1109), channel_id=1, source_target_pairs={{0,8},{8,16},{16,24},{24,32},{32,40},{40,48},{48,56},{56,64},{64,7... | collective-permute-start | bytes 4718600 | tf_op jit(solution)/shard_map/ppermute | solution.py:38
  174.3 37.3 %collective-permute-start.13 = (f32[2,96,2048]{2,1,0:T(8,128)S(1)}, f32[2,96,2048]{2,1,0:T(8,128)S(1)}, u32[]{:S(2)}, u32[]{:S(2)}) collective-permute-start(f32[2,96,2048]{2,1,0:T(8,128)S(1)} %copy-done.19), channel_id=1, source_target_pairs={{8,0},{16,8},{24,16},{32,24},{40,32},{48,40},{56,48},{64,56},{72,6... | collective-permute-start | bytes 4718600 | tf_op jit(solution)/shard_map/ppermute | solution.py:38
  178.0 33.7 %copy-start.8 = (f32[2,1,96,2048]{3,2,1,0:T(8,128)S(1)}, f32[2,1,96,2048]{3,2,1,0:T(8,128)}, u32[]{:S(2)}) copy-start(f32[2,1,96,2048]{3,2,1,0:T(8,128)} %param.6) | copy-start | bytes 4718596
  212.1 17.1 %copy-start = (f32[2,1,96,2048]{3,2,0,1:T(8,128)}, f32[2,1,96,2048]{3,2,0,1:T(8,128)S(1)}, u32[]{:S(2)}) copy-start(f32[2,1,96,2048]{3,2,0,1:T(8,128)S(1)} %bitcast_add_fusion) | copy-start | bytes 4718596
  212.2 5.5 %collective-permute-start.14 = (f32[2,1,4,2048]{3,2,0,1:T(4,128)S(1)}, f32[2,1,4,2048]{3,2,0,1:T(4,128)S(1)}, u32[]{:S(2)}, u32[]{:S(2)}) collective-permute-start(f32[2,1,4,2048]{3,2,0,1:T(4,128)S(1)} %get-tuple-element.95), channel_id=1, source_target_pairs={{0,1},{1,2},{2,3},{3,4},{4,5},{5,6},{6,7},{8,9},{9,10},{10,11},{11... | collective-permute-start | bytes 196616 | tf_op jit(solution)/shard_map/ppermute | solution.py:29
  215.5 5.6 %collective-permute-start.15 = (f32[2,1,4,2048]{3,2,0,1:T(4,128)S(1)}, f32[2,1,4,2048]{3,2,0,1:T(4,128)S(1)}, u32[]{:S(2)}, u32[]{:S(2)}) collective-permute-start(f32[2,1,4,2048]{3,2,0,1:T(4,128)S(1)} %get-tuple-element.96), channel_id=1, source_target_pairs={{1,0},{2,1},{3,2},{4,3},{5,4},{6,5},{7,6},{9,8},{10,9},{11,10},{12... | collective-permute-start | bytes 196616 | tf_op jit(solution)/shard_map/ppermute | solution.py:30
  227.6 1.6 copy-start.4
  230.7 1.2 copy-start.9
  238.8 17.9 %all-to-all-start.5 = ((f32[64,1,1]{2,1,0:T(1,128)}), f32[64,1,1]{2,1,0:T(1,128)S(1)}, u32[]{:S(2)}, u32[]{:S(2)}) async-start(f32[64,1,1]{2,1,0:T(1,128)} %broadcast_in_dim.23), calls=%async_computation.5 | async-start | bytes 65536 | tf_op jit(solution)/shard_map/all_to_all | solution.py:43
  258.0 1.9 copy-start.14
  260.0 6.0 %collective-permute-start.16 = (f32[2,2,1,4,2048]{4,3,1,2,0:T(4,128)S(1)}, f32[2,2,1,4,2048]{4,3,1,2,0:T(4,128)S(1)}, u32[]{:S(2)}, u32[]{:S(2)}) collective-permute-start(f32[2,2,1,4,2048]{4,3,1,2,0:T(4,128)S(1)} %get-tuple-element.32), channel_id=1, source_target_pairs={{0,1},{1,2},{2,3},{3,4},{4,5},{5,6},{6,7},{8,9},{9,10},{10,11},{11... | collective-permute-start | bytes 393224 | tf_op jit(solution)/shard_map/ppermute | solution.py:29
  263.9 6.3 %collective-permute-start.17 = (f32[2,2,1,4,2048]{4,3,1,2,0:T(4,128)S(1)}, f32[2,2,1,4,2048]{4,3,1,2,0:T(4,128)S(1)}, u32[]{:S(2)}, u32[]{:S(2)}) collective-permute-start(f32[2,2,1,4,2048]{4,3,1,2,0:T(4,128)S(1)} %get-tuple-element.33), channel_id=1, source_target_pairs={{1,0},{2,1},{3,2},{4,3},{5,4},{6,5},{7,6},{9,8},{10,9},{11,10},{12... | collective-permute-start | bytes 393224 | tf_op jit(solution)/shard_map/ppermute | solution.py:30
  272.0 1.4 copy-start.1
where the time goes:
time: 290 us; the launch traced here: 285 us
  waiting for transfers between devices  83.3 us (29%)
  other arithmetic  80.2 us (28%)
  starting transfers between devices  66.1 us (23%)
  blocking collectives  30.9 us (11%)
  local copies, waits for them, and re-layouts  20.7 us (7%)
  between operations  3.98 us (1%)
    ppermute x4, waiting for transfers between devices, shifted(): return lax.ppermute(x, axis, pairs)  61 us
    all_to_all x4, blocking collectives, from_everyone(): return lax.all_to_all(copies, axis, split_axis=0, concat_axis=0, tiled=True)  30.9 us
    ppermute x7, starting transfers between devices, extended(): before = lax.ppermute(last, axis, up)  27.9 us
    add x13, other arithmetic, advance(): return (offsets + STEP_SIZE * speeds, speeds)  15.5 us
    ppermute x7, waiting for transfers between devices, extended(): after = lax.ppermute(first, axis, down)  15.3 us
    all_to_all x2, starting transfers between devices, from_everyone(): return lax.all_to_all(copies, axis, split_axis=0, concat_axis=0, tiled=True)  15 us
    ppermute x7, starting transfers between devices, extended(): after = lax.ppermute(first, axis, down)  14.2 us
    another operation x5, other arithmetic, on_device(): state = extended(jnp.stack([offsets, speeds]), ((STRIP, 3),), SUBSTEPS)  12 us
  transfers between devices with their start and end apart: 20, of which 11 were waited for; matrix products, arithmetic and copies ran while one was open for 9% of the time, Pallas kernels for 0%

commit v1 on v0

v1 whole, which is shorter than its diff:
```python
import functools

import jax
import jax.numpy as jnp
from jax import lax
from jax.experimental import pallas as pl
from jax.experimental.pallas import tpu as pltpu
from jax.sharding import PartitionSpec as P

SPRING = 1.0
COUPLING = 0.5
STEP_SIZE = 0.4
DAMPING = 0.9
SPEED_CAP = 0.05
EPSILON = 1e-06
SUBSTEPS = 4

LINK = 0.5 * SPRING * STEP_SIZE * STEP_SIZE
PULL = COUPLING * STEP_SIZE * STEP_SIZE

HALO = 8
SUB = 8
LANES = 128
WIDE = 2
MESH = pl.DeviceIdType.MESH


def vreg_iota(axis):
    return lax.broadcasted_iota(jnp.int32, (SUB, LANES), axis)


def kernel(
    ns, nz, rows, tiles_c,
    u0, flow, fixed, links_a, links_d, out_u, out_v,
    sa, sb, sc, tgt, coef, raw, fl, sd, rx, carry, acc, mine, red1, red2,
    ld_u, ld_f, ld_g, e_snd, e_rcv, th_snd, th_rcv, h0_snd, h0_rcv, h1_snd, h1_rcv,
    r1_snd, r1_rcv, r2_snd, r2_rcv, out_sem,
):
    nc = tiles_c // WIDE
    nt = (rows + 2 * HALO) // SUB
    sec = lax.axis_index("sec")
    strip = lax.axis_index("strip")
    sec_up, sec_dn = lax.rem(sec + 1, ns), lax.rem(sec + ns - 1, ns)
    has_above_strip, has_below_strip = strip > 0, strip < nz - 1
    own = pl.ds(HALO, rows)

    def start_u(j, _):
        cols = pl.ds(pl.multiple_of(j * LANES, LANES), LANES)
        pltpu.make_async_copy(u0.at[:, 0, :, cols], sa.at[0:2, j, own, :], ld_u.at[j]).start()
        pltpu.make_async_copy(flow.at[:, 0, :, cols], fl.at[:, j], ld_f.at[j]).start()
        return 0

    def start_g(j, _):
        cols = pl.ds(pl.multiple_of(j * LANES, LANES), LANES)
        for n, ref in enumerate((links_a, links_d, fixed)):
            pltpu.make_async_copy(ref.at[0, :, cols], raw.at[n, j, own, :], ld_g.at[n, j]).start()
        return 0

    lax.fori_loop(0, tiles_c, start_u, 0)
    lax.fori_loop(0, tiles_c, start_g, 0)

    barrier = pltpu.get_barrier_semaphore()

    def greet_strip(d, _):
        pl.semaphore_signal(barrier, inc=1, device_id={"strip": lax.rem(strip + d, nz)}, device_id_type=MESH)
        return 0

    def greet_sec(d, _):
        pl.semaphore_signal(barrier, inc=1, device_id={"sec": lax.rem(sec + d, ns)}, device_id_type=MESH)
        return 0

    lax.fori_loop(1, nz, greet_strip, 0)
    lax.fori_loop(1, ns, greet_sec, 0)

    zero = jnp.zeros((SUB, LANES), jnp.float32)
    zero_i = jnp.zeros((SUB, LANES), jnp.int32)

    def clear(at):
        def body(j, _):
            for n in range(3):
                raw[n, j, at, :] = zero_i
            for n in range(2):
                sa[n, j, at, :] = zero
                tgt[0, n, j, at, :] = zero
                tgt[1, n, j, at, :] = zero
            for n in range(4):
                sc[n, j, at, :] = zero
            return 0

        lax.fori_loop(0, tiles_c, body, 0)

    top_halo, bottom_halo = pl.ds(0, HALO), pl.ds(HALO + rows, HALO)
    top_own, bottom_own = pl.ds(HALO, HALO), pl.ds(rows, HALO)

    @pl.when(jnp.logical_not(has_above_strip))
    def _():
        clear(top_halo)

    @pl.when(jnp.logical_not(has_below_strip))
    def _():
        clear(bottom_halo)

    pl.semaphore_wait(barrier, nz - 1 + ns - 1)

    pieces = ((0, SUB), (rows - SUB, SUB), (SUB, rows - 2 * SUB))

    def e_copy(sweep, d, c, p, state):
        first, count = pieces[p]
        chunk = pl.ds(c * WIDE, WIDE)
        if d == 0:
            src = state.at[0:2, chunk, pl.ds(HALO + first, count), :]
        else:
            src = sd.at[sweep, :, chunk, pl.ds(first, count), :]
        return pltpu.make_async_remote_copy(
            src_ref=src,
            dst_ref=rx.at[sweep, d, :, chunk, pl.ds(first, count), :],
            send_sem=e_snd.at[sweep, d, c, p],
            recv_sem=e_rcv.at[sweep, d, c, p],
            device_id={"sec": sec_up if d == 0 else sec_dn},
            device_id_type=MESH,
        )

    def strip_copy(ref_of, d, snd, rcv):
        return pltpu.make_async_remote_copy(
            src_ref=ref_of(top_own if d == 0 else bottom_own),
            dst_ref=ref_of(bottom_halo if d == 0 else top_halo),
            send_sem=snd,
            recv_sem=rcv,
            device_id={"strip": strip + (-1 if d == 0 else 1)},
            device_id_type=MESH,
        )

    sends_to = (has_above_strip, has_below_strip)
    hears_from = (has_below_strip, has_above_strip)

    def strip_start(make):
        for d in range(2):
            @pl.when(sends_to[d])
            def _():
                make(d).start()

    def strip_wait_send(make):
        for d in range(2):
            @pl.when(sends_to[d])
            def _():
                make(d).wait_send()

    def strip_wait_recv(make):
        for d in range(2):
            @pl.when(hears_from[d])
            def _():
                make(d).wait_recv()

    def t_halo(sweep, c):
        chunk = pl.ds(c * WIDE, WIDE)
        return lambda d: strip_copy(
            lambda at: tgt.at[sweep, :, chunk, at, :], d, th_snd.at[sweep, d, c], th_rcv.at[sweep, d, c]
        )

    def u_halo(d):
        return strip_copy(lambda at: sa.at[0:2, :, at, :], d, h0_snd.at[0, d], h0_rcv.at[0, d])

    def raw_halo(d):
        return strip_copy(lambda at: raw.at[:, :, at, :], d, h0_snd.at[1, d], h0_rcv.at[1, d])

    def s_halo(c):
        chunk = pl.ds(c * WIDE, WIDE)
        return lambda d: strip_copy(
            lambda at: sc.at[:, chunk, at, :], d, h1_snd.at[d, c], h1_rcv.at[d, c]
        )

    def make_down(sweep, c, state):
        for jj in range(WIDE):
            j = c * WIDE + jj
            for n in range(2):
                sd[sweep, n, j] = state[n, j, own, :] - fl[n, j]

    def e_send(sweep, c, state):
        for d in range(2):
            for p in range(3):
                e_copy(sweep, d, c, p, state).start()

    def first_sends(c, _):
        for jj in range(WIDE):
            j = c * WIDE + jj
            cols = pl.ds(pl.multiple_of(j * LANES, LANES), LANES)
            pltpu.make_async_copy(u0.at[:, 0, :, cols], sa.at[0:2, j, own, :], ld_u.at[j]).wait()
            pltpu.make_async_copy(flow.at[:, 0, :, cols], fl.at[:, j], ld_f.at[j]).wait()
        make_down(0, c, sa)
        e_send(0, c, sa)
        return 0

    lax.fori_loop(0, nc, first_sends, 0)
    strip_start(u_halo)

    def wait_g(j, _):
        cols = pl.ds(pl.multiple_of(j * LANES, LANES), LANES)
        for n, ref in enumerate((links_a, links_d, fixed)):
            pltpu.make_async_copy(ref.at[0, :, cols], raw.at[n, j, own, :], ld_g.at[n, j]).wait()
        return 0

    lax.fori_loop(0, tiles_c, wait_g, 0)
    strip_start(raw_halo)
    strip_wait_recv(u_halo)
    strip_wait_recv(raw_halo)

    lane, sublane = vreg_iota(1), vreg_iota(0)
    first_lane, last_lane = lane == 0, lane == LANES - 1
    first_sub = sublane == 0

    def convert(j, _):
        edge = jnp.logical_and(last_lane, j == tiles_c - 1)
        for i in range(nt):
            at = pl.ds(SUB * i, SUB)
            a = raw[0, j, at, :].astype(jnp.float32) * LINK
            coef[0, j, at, :] = jnp.where(edge, 0.0, a)
            dn = raw[1, j, at, :].astype(jnp.float32) * LINK
            if SUB * i == rows:
                bottom = jnp.logical_and(sublane == SUB - 1, strip == nz - 1)
                dn = jnp.where(bottom, 0.0, dn)
            coef[1, j, at, :] = dn
            coef[2, j, at, :] = 1.0 - raw[2, j, at, :].astype(jnp.float32)
        return 0

    lax.fori_loop(0, tiles_c, convert, 0)

    has_below, has_above = sec > 0, sec < ns - 1
    links = has_below.astype(jnp.float32) + has_above.astype(jnp.float32)
    hold = jnp.full((SUB, LANES), PULL, jnp.float32) * links
    below_on = jnp.broadcast_to(has_below, (SUB, LANES))
    above_on = jnp.broadcast_to(has_above, (SUB, LANES))

    def make_target(sweep, c, first, count):
        for jj in range(WIDE):
            j = c * WIDE + jj
            for i in range(first // SUB, (first + count) // SUB):
                at = pl.ds(SUB * i, SUB)
                for n in range(2):
                    below = jnp.where(below_on, rx[sweep, 0, n, j, at, :] + fl[n, j, at, :], 0.0)
                    above = jnp.where(above_on, rx[sweep, 1, n, j, at, :], 0.0)
                    tgt[sweep, n, j, pl.ds(HALO + SUB * i, SUB), :] = (below + above) * PULL

    def level(k, c, src, dst, sweep, damping, own_rows, power, final):
        lo, hi = (HALO // SUB, nt - HALO // SUB) if own_rows else (0, nt)
        j0 = c * WIDE
        beyond = jnp.minimum(j0 + WIDE, tiles_c - 1)
        js = [j0 + jj for jj in range(WIDE)] + [beyond]
        up_x, up_y = [zero] * WIDE, [zero] * WIDE
        total = zero

        def down_pull(i, jj, ux, uy):
            after = pl.ds(SUB * i + 1, SUB)
            dx = src[0, js[jj], after, :] - ux
            dy = src[1, js[jj], after, :] - uy
            ey = dy + 1.0
            stretch = dx * dx + dy * (ey + 1.0)
            pull = stretch * coef[1, js[jj], pl.ds(SUB * i, SUB), :]
            return pull * dx, pull * ey

        if own_rows:
            at = pl.ds(SUB * (lo - 1), SUB)
            for jj in range(WIDE):
                hx, hy = down_pull(lo - 1, jj, src[0, js[jj], at, :], src[1, js[jj], at, :])
                up_x[jj], up_y[jj] = pltpu.roll(hx, 1, 0), pltpu.roll(hy, 1, 0)
        for i in range(lo, hi):
            at = pl.ds(SUB * i, SUB)
            ux = [src[0, j, at, :] for j in js]
            uy = [src[1, j, at, :] for j in js]
            turned_x = [pltpu.roll(u, LANES - 1, 1) for u in ux]
            turned_y = [pltpu.roll(u, LANES - 1, 1) for u in uy]
            left_x, left_y = carry[k, 0, at, :], carry[k, 1, at, :]
            for jj in range(WIDE):
                j = js[jj]
                dx = jnp.where(last_lane, turned_x[jj + 1], turned_x[jj]) - ux[jj]
                dy = jnp.where(last_lane, turned_y[jj + 1], turned_y[jj]) - uy[jj]
                ex = dx + 1.0
                pull = (dx * (ex + 1.0) + dy * dy) * coef[0, j, at, :]
                ax, ay = pull * ex, pull * dy
                gx, gy = pltpu.roll(ax, 1, 1), pltpu.roll(ay, 1, 1)
                fx = ax - jnp.where(first_lane, left_x, gx)
                fy = ay - jnp.where(first_lane, left_y, gy)
                left_x, left_y = gx, gy
                hx, hy = down_pull(i, jj, ux[jj], uy[jj])
                vx, vy = pltpu.roll(hx, 1, 0), pltpu.roll(hy, 1, 0)
                fx = fx + (hx - jnp.where(first_sub, up_x[jj], vx))
                fy = fy + (hy - jnp.where(first_sub, up_y[jj], vy))
                up_x[jj], up_y[jj] = vx, vy
                fx = fx + (tgt[sweep, 0, j, at, :] - hold * ux[jj])
                fy = fy + (tgt[sweep, 1, j, at, :] - hold * uy[jj])
                if damping is not None:
                    fx = fx + damping * src[2, j, at, :]
                    fy = fy + damping * src[3, j, at, :]
                mobility = coef[2, j, at, :]
                wx, wy = mobility * fx, mobility * fy
                dst[0, j, at, :] = ux[jj] + wx
                dst[1, j, at, :] = uy[jj] + wy
                if final:
                    dst[2, j, at, :] = wx * (1.0 / STEP_SIZE)
                    dst[3, j, at, :] = wy * (1.0 / STEP_SIZE)
                else:
                    dst[2, j, at, :] = wx
                    dst[3, j, at, :] = wy
                if power and HALO // SUB <= i < nt - HALO // SUB:
                    total = total + (wx * wx + wy * wy)
            carry[k, 0, at, :] = left_x
            carry[k, 1, at, :] = left_y
        if power:
            acc[...] += total

    def reset():
        for k in range(SUBSTEPS):
            for n in range(2):
                for i in range(nt):
                    carry[k, n, pl.ds(SUB * i, SUB), :] = zero
        acc[...] = zero

    def chunk_in(c):
        return jnp.logical_and(c >= 0, c < nc)

    entries = 2.0 * ns * nz * rows * tiles_c * LANES

    def spread_scale(n):
        mine[2 * n] = jnp.sum(acc[...], axis=0, keepdims=True)

        def to_strip(d):
            return pltpu.make_async_remote_copy(
                src_ref=mine.at[2 * n], dst_ref=red1.at[n, d - 1],
                send_sem=r1_snd.at[n, d - 1], recv_sem=r1_rcv.at[n, d - 1],
                device_id={"strip": lax.rem(strip + d, nz)}, device_id_type=MESH,
            )

        def to_sec(d):
            return pltpu.make_async_remote_copy(
                src_ref=mine.at[2 * n + 1], dst_ref=red2.at[n, d - 1],
                send_sem=r2_snd.at[n, d - 1], recv_sem=r2_rcv.at[n, d - 1],
                device_id={"sec": lax.rem(sec + d, ns)}, device_id_type=MESH,
            )

        for d in range(1, nz):
            to_strip(d).start()
        for d in range(1, nz):
            to_strip(d).wait_recv()
        mine[2 * n + 1] = mine[2 * n] + jnp.sum(red1[n], axis=0)
        for d in range(1, ns):
            to_sec(d).start()
        for d in range(1, ns):
            to_sec(d).wait_recv()
        whole = mine[2 * n + 1] + jnp.sum(red2[n], axis=0)
        for d in range(1, nz):
            to_strip(d).wait_send()
        for d in range(1, ns):
            to_sec(d).wait_send()
        power = jnp.sum(whole, axis=1, keepdims=True) * (1.0 / (STEP_SIZE * STEP_SIZE))
        spread = jnp.sqrt(power * (1.0 / entries) + EPSILON)
        scale = jnp.minimum(1.0, SPEED_CAP / spread)
        return jnp.broadcast_to(scale * DAMPING, (SUB, LANES))

    plain = DAMPING

    def wave(w, order, sweep, first_damping, own_rows, final=False, power=True, before=None):
        for k in range(SUBSTEPS):
            c = w - k
            last = k == SUBSTEPS - 1

            @pl.when(chunk_in(c))
            def _():
                if before is not None and k == 1:
                    before(c)
                level(
                    k, c, order[k], order[k + 1], sweep,
                    first_damping if k == 0 else plain,
                    own_rows and last, power and last, final and last,
                )

    def targets(w, sweep, state):
        @pl.when(w < nc)
        def _():
            for p in range(2):
                for d in range(2):
                    e_copy(sweep, d, w, p, state).wait_recv()
            for p in range(2):
                make_target(sweep, w, *pieces[p])
            strip_start(t_halo(sweep, w))

        @pl.when(chunk_in(w - 1))
        def _():
            c = w - 1
            for d in range(2):
                e_copy(sweep, d, c, 2, state).wait_recv()
            make_target(sweep, c, *pieces[2])
            strip_wait_recv(t_halo(sweep, c))

    def sent(sweep, state):
        def before(c):
            for d in range(2):
                for p in range(3):
                    e_copy(sweep, d, c, p, state).wait_send()
            if sweep == 1:
                strip_wait_send(s_halo(c))

        return before

    reset()
    strip_wait_send(u_halo)
    strip_wait_send(raw_halo)

    def round0(w, _):
        targets(w, 0, sa)
        wave(w - 1, (sa, sb, sa, sb, sa), 0, None, False, before=sent(0, sa))
        return 0

    lax.fori_loop(0, nc + SUBSTEPS, round0, 0)
    damping1 = spread_scale(0)

    reset()

    def round1(w, _):
        wave(w, (sa, sb, sa, sb, sc), 0, damping1, True)
        c = w - (SUBSTEPS - 1)

        @pl.when(chunk_in(c))
        def _():
            make_down(1, c, sc)
            strip_start(s_halo(c))
            e_send(1, c, sc)

        return 0

    lax.fori_loop(0, nc + SUBSTEPS - 1, round1, 0)
    damping2 = spread_scale(1)

    reset()

    def round2(w, _):
        @pl.when(w < nc)
        def _():
            strip_wait_recv(s_halo(w))

        targets(w, 1, sc)
        wave(w - 1, (sc, sb, sc, sb, sc), 1, damping2, False, before=sent(1, sc))
        return 0

    lax.fori_loop(0, nc + SUBSTEPS, round2, 0)
    damping3 = spread_scale(2)

    reset()

    def out_copies(j):
        cols = pl.ds(pl.multiple_of(j * LANES, LANES), LANES)
        return (
            pltpu.make_async_copy(sa.at[0:2, j, own, :], out_u.at[:, 0, :, cols], out_sem.at[0, j]),
            pltpu.make_async_copy(sa.at[2:4, j, own, :], out_v.at[:, 0, :, cols], out_sem.at[1, j]),
        )

    def round3(w, _):
        wave(w, (sc, sb, sc, sb, sa), 1, damping3, True, final=True, power=False)
        c = w - (SUBSTEPS - 1)

        @pl.when(chunk_in(c))
        def _():
            for jj in range(WIDE):
                for copy in out_copies(c * WIDE + jj):
                    copy.start()

        return 0

    lax.fori_loop(0, nc + SUBSTEPS - 1, round3, 0)

    def finish(c, _):
        strip_wait_send(t_halo(0, c))
        strip_wait_send(t_halo(1, c))
        for jj in range(WIDE):
            for copy in out_copies(c * WIDE + jj):
                copy.wait()
        return 0

    lax.fori_loop(0, nc, finish, 0)


def relax(mesh, start_offsets, section_flow, fixed_nodes, links_across, links_down):
    ns, nz = mesh.shape["sec"], mesh.shape["strip"]
    rows, columns = fixed_nodes.shape[1:]
    tiles_c = columns // LANES
    nc = tiles_c // WIDE
    padded = rows + 2 * HALO
    f32 = jnp.float32
    state = pltpu.VMEM((4, tiles_c, padded + SUB, LANES), f32)
    dma = pltpu.SemaphoreType.DMA
    out = jax.ShapeDtypeStruct(start_offsets.shape, f32)
    return pl.pallas_call(
        functools.partial(kernel, ns, nz, rows, tiles_c),
        out_shape=(out, out),
        in_specs=[pl.BlockSpec(memory_space=pl.ANY)] * 5,
        out_specs=(pl.BlockSpec(memory_space=pl.ANY), pl.BlockSpec(memory_space=pl.ANY)),
        scratch_shapes=[
            state, state, state,
            pltpu.VMEM((2, 2, tiles_c, padded, LANES), f32),
            pltpu.VMEM((3, tiles_c, padded, LANES), f32),
            pltpu.VMEM((3, tiles_c, padded, LANES), jnp.int32),
            pltpu.VMEM((2, tiles_c, rows, LANES), f32),
            pltpu.VMEM((2, 2, tiles_c, rows, LANES), f32),
            pltpu.VMEM((2, 2, 2, tiles_c, rows, LANES), f32),
            pltpu.VMEM((SUBSTEPS, 2, padded, LANES), f32),
            pltpu.VMEM((SUB, LANES), f32),
            pltpu.VMEM((6, 1, LANES), f32),
            pltpu.VMEM((3, nz - 1, 1, LANES), f32),
            pltpu.VMEM((3, ns - 1, 1, LANES), f32),
            dma((tiles_c,)), dma((tiles_c,)), dma((3, tiles_c)),
            dma((2, 2, nc, 3)), dma((2, 2, nc, 3)),
            dma((2, 2, nc)), dma((2, 2, nc)),
            dma((2, 2)), dma((2, 2)),
            dma((2, nc)), dma((2, nc)),
            dma((3, nz - 1)), dma((3, nz - 1)),
            dma((3, ns - 1)), dma((3, ns - 1)),
            dma((2, tiles_c)),
        ],
        compiler_params=pltpu.CompilerParams(
            collective_id=0, has_side_effects=True, vmem_limit_bytes=60 * 1024 * 1024
        ),
    )(start_offsets, section_flow, fixed_nodes, links_across, links_down)


def solution(mesh):
    whole = P(None, "sec", "strip", None)
    flags = P("sec", "strip", None)
    return jax.shard_map(
        functools.partial(relax, mesh),
        mesh=mesh,
        in_specs=(whole, whole, flags, flags, flags),
        out_specs=(whole, whole),
        check_vma=False,
    )
```

time: 290 us -> 143 us (0.49); the launches traced: 285 us -> 143 us
  Pallas kernels: 0 us -> 138 us
  waiting for transfers between devices: 83.3 us -> 0 us
  other arithmetic: 80.2 us -> 0 us
  starting transfers between devices: 66.1 us -> 0 us
  blocking collectives: 30.9 us -> 0 us
  local copies, waits for them, and re-layouts: 20.7 us -> 3.97 us
  between operations: 3.98 us -> 0.65 us
    pallas_call x0 -> x1, Pallas kernels: none -> 138 us  [relax(): pl.pallas_call(functools.partial(kernel, ns, nz, rows, tiles_c), out_shap...]
    ppermute x18 -> x0, waiting for transfers between devices: 76.3 us -> none  [the longest x4 61 us: shifted(): return lax.ppermute(x, axis, pairs)]
    ppermute x18 -> x0, starting transfers between devices: 51.1 us -> none  [the longest x7 27.9 us: extended(): before = lax.ppermute(last, axis, up)]
    all_to_all x4 -> x0, blocking collectives: 30.9 us -> none  [from_everyone(): return lax.all_to_all(copies, axis, split_axis=0, concat_axis=0, tiled=True)]
    another operation x39 -> x0, other arithmetic: 22.7 us -> none  [the longest x5 12 us: on_device(): state = extended(jnp.stack([offsets, speeds]), ((STRIP, 3),), SUBSTEPS)]
    mul x36 -> x0, other arithmetic: 21.2 us -> none  [the longest x16 8.38 us: spring_forces(): tension * across_x]
    add x15 -> x0, other arithmetic: 17.8 us -> none  [the longest x13 15.5 us: advance(): return (offsets + STEP_SIZE * speeds, speeds)]
    all_to_all x2 -> x0, starting transfers between devices: 15 us -> none  [from_everyone(): return lax.all_to_all(copies, axis, split_axis=0, concat_axis=0, tiled=True)]
  transfers between devices with their start and end apart: 20 -> 0, of which waited for: 11 -> 0; matrix products, arithmetic and copies ran while one was open for 9% -> 0% of each run, Pallas kernels for 0% -> 0%
where the time goes in v1:
time: 143 us
  Pallas kernels  138 us (97%)
  local copies, waits for them, and re-layouts  3.97 us (3%)
    pallas_call x1, Pallas kernels, relax(): pl.pallas_call(functools.partial(kernel, ns, nz, rows, tiles_c), out_shap...  138 us
    unnamed x4, local copies, waits for them, and re-layouts  3.97 us

profile of v1, /device:TPU:1, one launch (start us, length us, event | category | flops | bytes accessed | tf_op | source)
XLA Modules:
  0.0 142.6 jit_solution(9311446876896938791)
XLA Ops:
  0.6 138.0 %shard_map.68 = (f32[2,1,96,2048]{3,2,1,0:T(8,128)}, f32[2,1,96,2048]{3,2,1,0:T(8,128)}) custom-call(f32[2,1,96,2048]{3,2,1,0:T(8,128)} %u0.1, f32[2,1,96,2048]{3,2,1,0:T(8,128)} %flow.1, s32[1,96,2048]{2,1,0:T(8,128)} %fixed.1, s32[1,96,2048]{2,1,0:T(8,128)} %links_a.1, s32[1,96,2048]{2,1,0:T(8,128)} %links_d.1), custom_call_target="tpu_custom_call" | custom-call | tf_op jit(solution)/shard_map/pallas_call | solution.py:490
  138.6 0.0 copy-start
  138.6 2.8 %copy.9 = f32[2,1,96,2048]{3,2,1,0:T(8,128)} copy(f32[2,1,96,2048]{3,2,1,0:T(8,128)} %get-tuple-element.4) | data formatting | bytes 3145728
  141.4 0.0 copy-done
  141.5 1.1 copy.10
Async XLA Ops:
  138.6 2.8 %copy-start = (f32[2,1,96,2048]{3,2,1,0:T(8,128)S(1)}, f32[2,1,96,2048]{3,2,1,0:T(8,128)}, u32[]{:S(2)}) copy-start(f32[2,1,96,2048]{3,2,1,0:T(8,128)} %get-tuple-element.5) | copy-start | bytes 4718596

commit v2 on v1

--- a/solution.py
+++ b/solution.py
@@ -33,7 +33,7 @@
     ns, nz, rows, tiles_c,
     u0, flow, fixed, links_a, links_d, out_u, out_v,
     sa, sb, sc, tgt, coef, raw, fl, sd, rx, carry, acc, mine, red1, red2,
-    ld_u, ld_f, ld_g, e_snd, e_rcv, th_snd, th_rcv, h0_snd, h0_rcv, h1_snd, h1_rcv,
+    ld_s, ld_g, e_snd, e_rcv, th_snd, th_rcv, h0_snd, h0_rcv, h1_snd, h1_rcv,
     r1_snd, r1_rcv, r2_snd, r2_rcv, out_sem,
 ):
     nc = tiles_c // WIDE
@@ -44,16 +44,20 @@
     has_above_strip, has_below_strip = strip > 0, strip < nz - 1
     own = pl.ds(HALO, rows)
 
+    def wait_bytes(ref, sem):
+        pltpu.make_async_copy(ref, ref, sem).wait()
+
     def start_u(j, _):
         cols = pl.ds(pl.multiple_of(j * LANES, LANES), LANES)
-        pltpu.make_async_copy(u0.at[:, 0, :, cols], sa.at[0:2, j, own, :], ld_u.at[j]).start()
-        pltpu.make_async_copy(flow.at[:, 0, :, cols], fl.at[:, j], ld_f.at[j]).start()
+        sem = ld_s.at[j // WIDE]
+        pltpu.make_async_copy(u0.at[:, 0, :, cols], sa.at[0:2, j, own, :], sem).start()
+        pltpu.make_async_copy(flow.at[:, 0, :, cols], fl.at[:, j], sem).start()
         return 0
 
     def start_g(j, _):
         cols = pl.ds(pl.multiple_of(j * LANES, LANES), LANES)
         for n, ref in enumerate((links_a, links_d, fixed)):
-            pltpu.make_async_copy(ref.at[0, :, cols], raw.at[n, j, own, :], ld_g.at[n, j]).start()
+            pltpu.make_async_copy(ref.at[0, :, cols], raw.at[n, j, own, :], ld_g.at[0]).start()
         return 0
 
     lax.fori_loop(0, tiles_c, start_u, 0)
@@ -100,8 +104,6 @@
     def _():
         clear(bottom_halo)
 
-    pl.semaphore_wait(barrier, nz - 1 + ns - 1)
-
     pieces = ((0, SUB), (rows - SUB, SUB), (SUB, rows - 2 * SUB))
 
     def e_copy(sweep, d, c, p, state):
@@ -114,8 +116,8 @@
         return pltpu.make_async_remote_copy(
             src_ref=src,
             dst_ref=rx.at[sweep, d, :, chunk, pl.ds(first, count), :],
-            send_sem=e_snd.at[sweep, d, c, p],
-            recv_sem=e_rcv.at[sweep, d, c, p],
+            send_sem=e_snd.at[d, c],
+            recv_sem=e_rcv.at[d, c, p // 2],
             device_id={"sec": sec_up if d == 0 else sec_dn},
             device_id_type=MESH,
         )
@@ -154,7 +156,7 @@
     def t_halo(sweep, c):
         chunk = pl.ds(c * WIDE, WIDE)
         return lambda d: strip_copy(
-            lambda at: tgt.at[sweep, :, chunk, at, :], d, th_snd.at[sweep, d, c], th_rcv.at[sweep, d, c]
+            lambda at: tgt.at[sweep, :, chunk, at, :], d, th_snd.at[sweep, d], th_rcv.at[d, c]
         )
 
     def u_halo(d):
@@ -166,8 +168,14 @@
     def s_halo(c):
         chunk = pl.ds(c * WIDE, WIDE)
         return lambda d: strip_copy(
-            lambda at: sc.at[:, chunk, at, :], d, h1_snd.at[d, c], h1_rcv.at[d, c]
+            lambda at: sc.at[:, chunk, at, :], d, h1_snd.at[d], h1_rcv.at[d]
         )
+
+    def strip_wait_all(on, ref, sem):
+        for d in range(2):
+            @pl.when(on[d])
+            def _():
+                wait_bytes(ref, sem.at[d])
 
     def make_down(sweep, c, state):
         for jj in range(WIDE):
@@ -180,26 +188,22 @@
             for p in range(3):
                 e_copy(sweep, d, c, p, state).start()
 
+    def prepare(c):
+        wait_bytes(rx.at[0, :, :, pl.ds(c * WIDE, WIDE)], ld_s.at[c])
+        make_down(0, c, sa)
+
     def first_sends(c, _):
-        for jj in range(WIDE):
-            j = c * WIDE + jj
-            cols = pl.ds(pl.multiple_of(j * LANES, LANES), LANES)
-            pltpu.make_async_copy(u0.at[:, 0, :, cols], sa.at[0:2, j, own, :], ld_u.at[j]).wait()
-            pltpu.make_async_copy(flow.at[:, 0, :, cols], fl.at[:, j], ld_f.at[j]).wait()
-        make_down(0, c, sa)
+        prepare(c)
         e_send(0, c, sa)
         return 0
 
-    lax.fori_loop(0, nc, first_sends, 0)
+    prepare(0)
+    pl.semaphore_wait(barrier, nz - 1 + ns - 1)
+    e_send(0, 0, sa)
+    lax.fori_loop(1, nc, first_sends, 0)
     strip_start(u_halo)
 
-    def wait_g(j, _):
-        cols = pl.ds(pl.multiple_of(j * LANES, LANES), LANES)
-        for n, ref in enumerate((links_a, links_d, fixed)):
-            pltpu.make_async_copy(ref.at[0, :, cols], raw.at[n, j, own, :], ld_g.at[n, j]).wait()
-        return 0
-
-    lax.fori_loop(0, tiles_c, wait_g, 0)
+    wait_bytes(raw.at[:, :, own, :], ld_g.at[0])
     strip_start(raw_halo)
     strip_wait_recv(u_halo)
     strip_wait_recv(raw_halo)
@@ -319,37 +323,30 @@
 
     entries = 2.0 * ns * nz * rows * tiles_c * LANES
 
-    def spread_scale(n):
+    def spread_scale(n, first_sent=None, second_sent=None):
         mine[2 * n] = jnp.sum(acc[...], axis=0, keepdims=True)
-
-        def to_strip(d):
-            return pltpu.make_async_remote_copy(
+        for d in range(1, nz):
+            pltpu.make_async_remote_copy(
                 src_ref=mine.at[2 * n], dst_ref=red1.at[n, d - 1],
-                send_sem=r1_snd.at[n, d - 1], recv_sem=r1_rcv.at[n, d - 1],
+                send_sem=r1_snd.at[n], recv_sem=r1_rcv.at[n],
                 device_id={"strip": lax.rem(strip + d, nz)}, device_id_type=MESH,
-            )
-
-        def to_sec(d):
-            return pltpu.make_async_remote_copy(
+            ).start()
+        if first_sent is not None:
+            first_sent()
+        wait_bytes(red1.at[n], r1_rcv.at[n])
+        mine[2 * n + 1] = mine[2 * n] + jnp.sum(red1[n], axis=0)
+        for d in range(ns - 1, 0, -1):
+            pltpu.make_async_remote_copy(
                 src_ref=mine.at[2 * n + 1], dst_ref=red2.at[n, d - 1],
-                send_sem=r2_snd.at[n, d - 1], recv_sem=r2_rcv.at[n, d - 1],
+                send_sem=r2_snd.at[n], recv_sem=r2_rcv.at[n],
                 device_id={"sec": lax.rem(sec + d, ns)}, device_id_type=MESH,
-            )
-
-        for d in range(1, nz):
-            to_strip(d).start()
-        for d in range(1, nz):
-            to_strip(d).wait_recv()
-        mine[2 * n + 1] = mine[2 * n] + jnp.sum(red1[n], axis=0)
-        for d in range(1, ns):
-            to_sec(d).start()
-        for d in range(1, ns):
-            to_sec(d).wait_recv()
+            ).start()
+        if second_sent is not None:
+            second_sent()
+        wait_bytes(red2.at[n], r2_rcv.at[n])
         whole = mine[2 * n + 1] + jnp.sum(red2[n], axis=0)
-        for d in range(1, nz):
-            to_strip(d).wait_send()
-        for d in range(1, ns):
-            to_sec(d).wait_send()
+        wait_bytes(red1.at[n], r1_snd.at[n])
+        wait_bytes(red2.at[n], r2_snd.at[n])
         power = jnp.sum(whole, axis=1, keepdims=True) * (1.0 / (STEP_SIZE * STEP_SIZE))
         spread = jnp.sqrt(power * (1.0 / entries) + EPSILON)
         scale = jnp.minimum(1.0, SPEED_CAP / spread)
@@ -372,31 +369,25 @@
                     own_rows and last, power and last, final and last,
                 )
 
-    def targets(w, sweep, state):
-        @pl.when(w < nc)
-        def _():
-            for p in range(2):
-                for d in range(2):
-                    e_copy(sweep, d, w, p, state).wait_recv()
-            for p in range(2):
-                make_target(sweep, w, *pieces[p])
-            strip_start(t_halo(sweep, w))
-
-        @pl.when(chunk_in(w - 1))
-        def _():
-            c = w - 1
-            for d in range(2):
-                e_copy(sweep, d, c, 2, state).wait_recv()
-            make_target(sweep, c, *pieces[2])
-            strip_wait_recv(t_halo(sweep, c))
-
-    def sent(sweep, state):
+    def boundary(sweep, c):
+        for d in range(2):
+            wait_bytes(rx.at[sweep, d, :, pl.ds(c * WIDE, WIDE), pl.ds(0, 2 * SUB)], e_rcv.at[d, c, 0])
+        for p in range(2):
+            make_target(sweep, c, *pieces[p])
+        strip_start(t_halo(sweep, c))
+
+    def interior(sweep, c):
+        for d in range(2):
+            wait_bytes(
+                rx.at[sweep, d, :, pl.ds(c * WIDE, WIDE), pl.ds(SUB, rows - 2 * SUB)], e_rcv.at[d, c, 1]
+            )
+        make_target(sweep, c, *pieces[2])
+        strip_wait_recv(t_halo(sweep, c))
+
+    def sent(sweep):
         def before(c):
             for d in range(2):
-                for p in range(3):
-                    e_copy(sweep, d, c, p, state).wait_send()
-            if sweep == 1:
-                strip_wait_send(s_halo(c))
+                wait_bytes(rx.at[sweep, d, :, pl.ds(c * WIDE, WIDE)], e_snd.at[d, c])
 
         return before
 
@@ -405,14 +396,22 @@
     strip_wait_send(raw_halo)
 
     def round0(w, _):
-        targets(w, 0, sa)
-        wave(w - 1, (sa, sb, sa, sb, sa), 0, None, False, before=sent(0, sa))
+        @pl.when(w < nc)
+        def _():
+            boundary(0, w)
+
+        @pl.when(chunk_in(w - 1))
+        def _():
+            interior(0, w - 1)
+
+        wave(w - 1, (sa, sb, sa, sb, sa), 0, None, False, before=sent(0))
         return 0
 
     lax.fori_loop(0, nc + SUBSTEPS, round0, 0)
     damping1 = spread_scale(0)
 
     reset()
+    soon, ahead = min(3, nc), min(4, nc)
 
     def round1(w, _):
         wave(w, (sa, sb, sa, sb, sc), 0, damping1, True)
@@ -422,22 +421,47 @@
         def _():
             make_down(1, c, sc)
             strip_start(s_halo(c))
+
+        @pl.when(jnp.logical_and(c >= 0, c < soon))
+        def _():
             e_send(1, c, sc)
 
         return 0
 
     lax.fori_loop(0, nc + SUBSTEPS - 1, round1, 0)
-    damping2 = spread_scale(1)
+
+    def send_next():
+        for c in range(soon, ahead):
+            e_send(1, c, sc)
+
+    def send_rest():
+        def body(c, _):
+            e_send(1, c, sc)
+            return 0
+
+        def early(c, _):
+            boundary(1, c)
+            return 0
+
+        lax.fori_loop(ahead, nc, body, 0)
+        lax.fori_loop(0, ahead, early, 0)
+
+    damping2 = spread_scale(1, send_next, send_rest)
 
     reset()
+    strip_wait_all(hears_from, sc.at[:, :, top_halo, :], h1_rcv)
+    strip_wait_all(sends_to, sc.at[:, :, top_halo, :], h1_snd)
 
     def round2(w, _):
-        @pl.when(w < nc)
-        def _():
-            strip_wait_recv(s_halo(w))
-
-        targets(w, 1, sc)
-        wave(w - 1, (sc, sb, sc, sb, sc), 1, damping2, False, before=sent(1, sc))
+        @pl.when(jnp.logical_and(w >= ahead, w < nc))
+        def _():
+            boundary(1, w)
+
+        @pl.when(chunk_in(w - 1))
+        def _():
+            interior(1, w - 1)
+
+        wave(w - 1, (sc, sb, sc, sb, sc), 1, damping2, False, before=sent(1))
         return 0
 
     lax.fori_loop(0, nc + SUBSTEPS, round2, 0)
@@ -448,8 +472,8 @@
     def out_copies(j):
         cols = pl.ds(pl.multiple_of(j * LANES, LANES), LANES)
         return (
-            pltpu.make_async_copy(sa.at[0:2, j, own, :], out_u.at[:, 0, :, cols], out_sem.at[0, j]),
-            pltpu.make_async_copy(sa.at[2:4, j, own, :], out_v.at[:, 0, :, cols], out_sem.at[1, j]),
+            pltpu.make_async_copy(sa.at[0:2, j, own, :], out_u.at[:, 0, :, cols], out_sem.at[0]),
+            pltpu.make_async_copy(sa.at[2:4, j, own, :], out_v.at[:, 0, :, cols], out_sem.at[0]),
         )
 
     def round3(w, _):
@@ -466,15 +490,9 @@
 
     lax.fori_loop(0, nc + SUBSTEPS - 1, round3, 0)
 
-    def finish(c, _):
-        strip_wait_send(t_halo(0, c))
-        strip_wait_send(t_halo(1, c))
-        for jj in range(WIDE):
-            for copy in out_copies(c * WIDE + jj):
-                copy.wait()
-        return 0
-
-    lax.fori_loop(0, nc, finish, 0)
+    for sweep in range(2):
+        strip_wait_all(sends_to, tgt.at[sweep, :, :, top_halo, :], th_snd.at[sweep])
+    wait_bytes(sa.at[:, :, own, :], out_sem.at[0])
 
 
 def relax(mesh, start_offsets, section_flow, fixed_nodes, links_across, links_down):
@@ -505,14 +523,13 @@
             pltpu.VMEM((6, 1, LANES), f32),
             pltpu.VMEM((3, nz - 1, 1, LANES), f32),
             pltpu.VMEM((3, ns - 1, 1, LANES), f32),
-            dma((tiles_c,)), dma((tiles_c,)), dma((3, tiles_c)),
-            dma((2, 2, nc, 3)), dma((2, 2, nc, 3)),
-            dma((2, 2, nc)), dma((2, 2, nc)),
+            dma((nc,)), dma((1,)),
+            dma((2, nc)), dma((2, nc, 2)),
+            dma((2, 2)), dma((2, nc)),
             dma((2, 2)), dma((2, 2)),
-            dma((2, nc)), dma((2, nc)),
-            dma((3, nz - 1)), dma((3, nz - 1)),
-            dma((3, ns - 1)), dma((3, ns - 1)),
-            dma((2, tiles_c)),
+            dma((2,)), dma((2,)),
+            dma((3,)), dma((3,)), dma((3,)), dma((3,)),
+            dma((1,)),
         ],
         compiler_params=pltpu.CompilerParams(
             collective_id=0, has_side_effects=True, vmem_limit_bytes=60 * 1024 * 1024

time: 143 us -> 124 us (0.87)
  Pallas kernels: 138 us -> 120 us
    pallas_call x1, Pallas kernels: 138 us -> 120 us  [relax(): pl.pallas_call(functools.partial(kernel, ns, nz, rows, tiles_c), out_shap...]
where the time goes in v2:
time: 124 us
  Pallas kernels  120 us (97%)
  local copies, waits for them, and re-layouts  3.97 us (3%)
    pallas_call x1, Pallas kernels, relax(): pl.pallas_call(functools.partial(kernel, ns, nz, rows, tiles_c), out_shap...  120 us
    unnamed x4, local copies, waits for them, and re-layouts  3.97 us

profile of v2, /device:TPU:1, one launch (start us, length us, event | category | flops | bytes accessed | tf_op | source)
XLA Modules:
  0.0 124.2 jit_solution(3158027168201672362)
XLA Ops:
  0.6 119.6 %shard_map.68 = (f32[2,1,96,2048]{3,2,1,0:T(8,128)}, f32[2,1,96,2048]{3,2,1,0:T(8,128)}) custom-call(f32[2,1,96,2048]{3,2,1,0:T(8,128)} %u0.1, f32[2,1,96,2048]{3,2,1,0:T(8,128)} %flow.1, s32[1,96,2048]{2,1,0:T(8,128)} %fixed.1, s32[1,96,2048]{2,1,0:T(8,128)} %links_a.1, s32[1,96,2048]{2,1,0:T(8,128)} %links_d.1), custom_call_target="tpu_custom_call" | custom-call | tf_op jit(solution)/shard_map/pallas_call | solution.py:508
  120.2 0.0 copy-start
  120.2 2.8 %copy.9 = f32[2,1,96,2048]{3,2,1,0:T(8,128)} copy(f32[2,1,96,2048]{3,2,1,0:T(8,128)} %get-tuple-element.4) | data formatting | bytes 3145728
  123.0 0.0 copy-done
  123.1 1.1 copy.10
Async XLA Ops:
  120.2 2.8 %copy-start = (f32[2,1,96,2048]{3,2,1,0:T(8,128)S(1)}, f32[2,1,96,2048]{3,2,1,0:T(8,128)}, u32[]{:S(2)}) copy-start(f32[2,1,96,2048]{3,2,1,0:T(8,128)} %get-tuple-element.5) | copy-start | bytes 4718596

commit v3 on v2

--- a/solution.py
+++ b/solution.py
@@ -22,6 +22,7 @@
 SUB = 8
 LANES = 128
 WIDE = 2
+HALF = LANES // 2
 MESH = pl.DeviceIdType.MESH
 
 
@@ -29,12 +30,144 @@
     return lax.broadcasted_iota(jnp.int32, (SUB, LANES), axis)
 
 
+def pick(x, index):
+    return jnp.take_along_axis(x, index, axis=1, mode="promise_in_bounds")
+
+
+def split_columns(first, second):
+    lane = vreg_iota(1)
+    low = lane < HALF
+    a = pick(first, jnp.where(low, 2 * lane, 2 * lane - (LANES - 1)))
+    b = pick(second, jnp.where(low, 2 * lane + 1, 2 * lane - LANES))
+    return jnp.where(low, a, b), pltpu.roll(jnp.where(low, b, a), HALF, 1)
+
+
+def join_columns(even, odd):
+    lane = vreg_iota(1)
+    low = lane < HALF
+    half = lax.shift_right_logical(lane, 1)
+    is_even = lax.bitwise_and(lane, 1) == 0
+    turned = pltpu.roll(odd, HALF, 1)
+    first = pick(jnp.where(low, even, turned), jnp.where(is_even, half, half + HALF))
+    second = pick(jnp.where(low, turned, even), jnp.where(is_even, half + HALF, half))
+    return first, second
+
+
+def substeps(rows, tiles_c, coef, carry, acc, hold):
+    nc = tiles_c // WIDE
+    nt = (rows + 2 * HALO) // SUB
+    zero = jnp.zeros((SUB, LANES), jnp.float32)
+    lane, sublane = vreg_iota(1), vreg_iota(0)
+    first_lane, first_sub = lane == 0, sublane == 0
+
+    def level(k, c, src, dst, tgt, damping, own_rows, power=False, mode="step"):
+        lo, hi = (HALO // SUB, nt - HALO // SUB) if own_rows else (0, nt)
+        j0 = c * WIDE
+        beyond = jnp.minimum(j0 + WIDE, tiles_c - WIDE)
+        js = [j0, j0 + 1]
+        up_x, up_y = [zero] * WIDE, [zero] * WIDE
+        total = zero
+
+        def down_pull(i, jj, ux, uy):
+            after = pl.ds(SUB * i + 1, SUB)
+            dx = src[0, js[jj], after, :] - ux
+            dy = src[1, js[jj], after, :] - uy
+            ey = dy + 1.0
+            stretch = dx * dx + dy * (ey + 1.0)
+            pull = stretch * coef[1, js[jj], pl.ds(SUB * i, SUB), :]
+            return pull * dx, pull * ey
+
+        if own_rows:
+            at = pl.ds(SUB * (lo - 1), SUB)
+            for jj in range(WIDE):
+                hx, hy = down_pull(lo - 1, jj, src[0, js[jj], at, :], src[1, js[jj], at, :])
+                up_x[jj], up_y[jj] = pltpu.roll(hx, 1, 0), pltpu.roll(hy, 1, 0)
+        for i in range(lo, hi):
+            at = pl.ds(SUB * i, SUB)
+            ux = [src[0, j, at, :] for j in js]
+            uy = [src[1, j, at, :] for j in js]
+            right_x = (ux[1], pltpu.roll(jnp.where(first_lane, src[0, beyond, at, :], ux[0]), LANES - 1, 1))
+            right_y = (uy[1], pltpu.roll(jnp.where(first_lane, src[1, beyond, at, :], uy[0]), LANES - 1, 1))
+            pull_x, pull_y = [], []
+            for jj in range(WIDE):
+                dx, dy = right_x[jj] - ux[jj], right_y[jj] - uy[jj]
+                ex = dx + 1.0
+                pull = (dx * (ex + 1.0) + dy * dy) * coef[0, js[jj], at, :]
+                pull_x.append(pull * ex)
+                pull_y.append(pull * dy)
+            gx, gy = pltpu.roll(pull_x[1], 1, 1), pltpu.roll(pull_y[1], 1, 1)
+            left_x = (jnp.where(first_lane, carry[k, 0, at, :], gx), pull_x[0])
+            left_y = (jnp.where(first_lane, carry[k, 1, at, :], gy), pull_y[0])
+            carry[k, 0, at, :] = gx
+            carry[k, 1, at, :] = gy
+            done = []
+            for jj in range(WIDE):
+                j = js[jj]
+                fx = pull_x[jj] - left_x[jj]
+                fy = pull_y[jj] - left_y[jj]
+                hx, hy = down_pull(i, jj, ux[jj], uy[jj])
+                vx, vy = pltpu.roll(hx, 1, 0), pltpu.roll(hy, 1, 0)
+                fx = fx + (hx - jnp.where(first_sub, up_x[jj], vx))
+                fy = fy + (hy - jnp.where(first_sub, up_y[jj], vy))
+                up_x[jj], up_y[jj] = vx, vy
+                fx = fx + (tgt[0, j, at, :] - hold * ux[jj])
+                fy = fy + (tgt[1, j, at, :] - hold * uy[jj])
+                if damping is not None:
+                    fx = fx + damping * src[2, j, at, :]
+                    fy = fy + damping * src[3, j, at, :]
+                if mode == "pre":
+                    dst[0, j, at, :] = fx
+                    dst[1, j, at, :] = fy
+                    continue
+                mobility = coef[2, j, at, :]
+                wx, wy = mobility * fx, mobility * fy
+                new = (ux[jj] + wx, uy[jj] + wy)
+                if mode == "final":
+                    done.append(new + (wx * (1.0 / STEP_SIZE), wy * (1.0 / STEP_SIZE)))
+                else:
+                    for n, x in enumerate(new + (wx, wy)):
+                        dst[n, j, at, :] = x
+                if power and HALO // SUB <= i < nt - HALO // SUB:
+                    total = total + (wx * wx + wy * wy)
+            if mode == "final":
+                for n in range(4):
+                    for jj, x in enumerate(join_columns(done[0][n], done[1][n])):
+                        dst[n // 2, n % 2, js[jj], pl.ds(SUB * i - HALO, SUB), :] = x
+        if power:
+            acc[...] += total
+
+    def apply(c, src, pre, dst, damping):
+        for i in range(nt):
+            at = pl.ds(SUB * i, SUB)
+            for jj in range(WIDE):
+                j = c * WIDE + jj
+                for n in range(2):
+                    w = coef[2, j, at, :] * (pre[n, j, at, :] + damping * src[2 + n, j, at, :])
+                    dst[n, j, at, :] = src[n, j, at, :] + w
+                    dst[2 + n, j, at, :] = w
+
+    return level, apply
+
+
+def clear_carry(carry, rows):
+    zero = jnp.zeros((SUB, LANES), jnp.float32)
+    for k in range(SUBSTEPS):
+        for n in range(2):
+            for i in range((rows + 2 * HALO) // SUB):
+                carry[k, n, pl.ds(SUB * i, SUB), :] = zero
+
+
+def pull_of(sec, ns):
+    links = (sec > 0).astype(jnp.float32) + (sec < ns - 1).astype(jnp.float32)
+    return jnp.full((SUB, LANES), PULL, jnp.float32) * links
+
+
 def kernel(
     ns, nz, rows, tiles_c,
-    u0, flow, fixed, links_a, links_d, out_u, out_v,
-    sa, sb, sc, tgt, coef, raw, fl, sd, rx, carry, acc, mine, red1, red2,
+    u0, flow, fixed, links_a, links_d, sc, tgt1, coef, pre, damping_out,
+    sa, sb, tgt0, raw, fl, sd, rx, carry, acc, mine, red1, red2,
     ld_s, ld_g, e_snd, e_rcv, th_snd, th_rcv, h0_snd, h0_rcv, h1_snd, h1_rcv,
-    r1_snd, r1_rcv, r2_snd, r2_rcv, out_sem,
+    r1_snd, r1_rcv, r2_snd, r2_rcv,
 ):
     nc = tiles_c // WIDE
     nt = (rows + 2 * HALO) // SUB
@@ -43,6 +176,7 @@
     sec_up, sec_dn = lax.rem(sec + 1, ns), lax.rem(sec + ns - 1, ns)
     has_above_strip, has_below_strip = strip > 0, strip < nz - 1
     own = pl.ds(HALO, rows)
+    tgt = (tgt0, tgt1)
 
     def wait_bytes(ref, sem):
         pltpu.make_async_copy(ref, ref, sem).wait()
@@ -50,8 +184,8 @@
     def start_u(j, _):
         cols = pl.ds(pl.multiple_of(j * LANES, LANES), LANES)
         sem = ld_s.at[j // WIDE]
-        pltpu.make_async_copy(u0.at[:, 0, :, cols], sa.at[0:2, j, own, :], sem).start()
-        pltpu.make_async_copy(flow.at[:, 0, :, cols], fl.at[:, j], sem).start()
+        pltpu.make_async_copy(u0.at[:, 0, :, cols], sb.at[0:2, j, own, :], sem).start()
+        pltpu.make_async_copy(flow.at[:, 0, :, cols], sb.at[2:4, j, own, :], sem).start()
         return 0
 
     def start_g(j, _):
@@ -85,8 +219,8 @@
                 raw[n, j, at, :] = zero_i
             for n in range(2):
                 sa[n, j, at, :] = zero
-                tgt[0, n, j, at, :] = zero
-                tgt[1, n, j, at, :] = zero
+                tgt0[n, j, at, :] = zero
+                tgt1[n, j, at, :] = zero
             for n in range(4):
                 sc[n, j, at, :] = zero
             return 0
@@ -156,7 +290,7 @@
     def t_halo(sweep, c):
         chunk = pl.ds(c * WIDE, WIDE)
         return lambda d: strip_copy(
-            lambda at: tgt.at[sweep, :, chunk, at, :], d, th_snd.at[sweep, d], th_rcv.at[d, c]
+            lambda at: tgt[sweep].at[:, chunk, at, :], d, th_snd.at[sweep, d], th_rcv.at[d, c]
         )
 
     def u_halo(d):
@@ -190,7 +324,16 @@
 
     def prepare(c):
         wait_bytes(rx.at[0, :, :, pl.ds(c * WIDE, WIDE)], ld_s.at[c])
-        make_down(0, c, sa)
+        j = c * WIDE
+        for i in range(rows // SUB):
+            wide, at = pl.ds(HALO + SUB * i, SUB), pl.ds(SUB * i, SUB)
+            for n in range(2):
+                u = split_columns(sb[n, j, wide, :], sb[n, j + 1, wide, :])
+                f = split_columns(sb[2 + n, j, wide, :], sb[2 + n, j + 1, wide, :])
+                for jj in range(WIDE):
+                    sa[n, j + jj, wide, :] = u[jj]
+                    fl[n, j + jj, at, :] = f[jj]
+                    sd[0, n, j + jj, at, :] = u[jj] - f[jj]
 
     def first_sends(c, _):
         prepare(c)
@@ -212,25 +355,29 @@
     first_lane, last_lane = lane == 0, lane == LANES - 1
     first_sub = sublane == 0
 
-    def convert(j, _):
-        edge = jnp.logical_and(last_lane, j == tiles_c - 1)
+    def convert(c, _):
+        j = c * WIDE
+        edge = jnp.logical_and(last_lane, c == nc - 1)
         for i in range(nt):
             at = pl.ds(SUB * i, SUB)
-            a = raw[0, j, at, :].astype(jnp.float32) * LINK
-            coef[0, j, at, :] = jnp.where(edge, 0.0, a)
-            dn = raw[1, j, at, :].astype(jnp.float32) * LINK
-            if SUB * i == rows:
-                bottom = jnp.logical_and(sublane == SUB - 1, strip == nz - 1)
-                dn = jnp.where(bottom, 0.0, dn)
-            coef[1, j, at, :] = dn
-            coef[2, j, at, :] = 1.0 - raw[2, j, at, :].astype(jnp.float32)
-        return 0
-
-    lax.fori_loop(0, tiles_c, convert, 0)
+            for n in range(3):
+                parts = split_columns(
+                    raw[n, j, at, :].astype(jnp.float32), raw[n, j + 1, at, :].astype(jnp.float32)
+                )
+                for jj in range(WIDE):
+                    x = 1.0 - parts[jj] if n == 2 else parts[jj] * LINK
+                    if n == 0 and jj == 1:
+                        x = jnp.where(edge, 0.0, x)
+                    if n == 1 and SUB * i == rows:
+                        bottom = jnp.logical_and(sublane == SUB - 1, strip == nz - 1)
+                        x = jnp.where(bottom, 0.0, x)
+                    coef[n, j + jj, at, :] = x
+        return 0
+
+    lax.fori_loop(0, nc, convert, 0)
 
     has_below, has_above = sec > 0, sec < ns - 1
-    links = has_below.astype(jnp.float32) + has_above.astype(jnp.float32)
-    hold = jnp.full((SUB, LANES), PULL, jnp.float32) * links
+    hold = pull_of(sec, ns)
     below_on = jnp.broadcast_to(has_below, (SUB, LANES))
     above_on = jnp.broadcast_to(has_above, (SUB, LANES))
 
@@ -242,81 +389,21 @@
                 for n in range(2):
                     below = jnp.where(below_on, rx[sweep, 0, n, j, at, :] + fl[n, j, at, :], 0.0)
                     above = jnp.where(above_on, rx[sweep, 1, n, j, at, :], 0.0)
-                    tgt[sweep, n, j, pl.ds(HALO + SUB * i, SUB), :] = (below + above) * PULL
-
-    def level(k, c, src, dst, sweep, damping, own_rows, power, final):
-        lo, hi = (HALO // SUB, nt - HALO // SUB) if own_rows else (0, nt)
-        j0 = c * WIDE
-        beyond = jnp.minimum(j0 + WIDE, tiles_c - 1)
-        js = [j0 + jj for jj in range(WIDE)] + [beyond]
-        up_x, up_y = [zero] * WIDE, [zero] * WIDE
-        total = zero
-
-        def down_pull(i, jj, ux, uy):
-            after = pl.ds(SUB * i + 1, SUB)
-            dx = src[0, js[jj], after, :] - ux
-            dy = src[1, js[jj], after, :] - uy
-            ey = dy + 1.0
-            stretch = dx * dx + dy * (ey + 1.0)
-            pull = stretch * coef[1, js[jj], pl.ds(SUB * i, SUB), :]
-            return pull * dx, pull * ey
-
-        if own_rows:
-            at = pl.ds(SUB * (lo - 1), SUB)
-            for jj in range(WIDE):
-                hx, hy = down_pull(lo - 1, jj, src[0, js[jj], at, :], src[1, js[jj], at, :])
-                up_x[jj], up_y[jj] = pltpu.roll(hx, 1, 0), pltpu.roll(hy, 1, 0)
-        for i in range(lo, hi):
-            at = pl.ds(SUB * i, SUB)
-            ux = [src[0, j, at, :] for j in js]
-            uy = [src[1, j, at, :] for j in js]
-            turned_x = [pltpu.roll(u, LANES - 1, 1) for u in ux]
-            turned_y = [pltpu.roll(u, LANES - 1, 1) for u in uy]
-            left_x, left_y = carry[k, 0, at, :], carry[k, 1, at, :]
-            for jj in range(WIDE):
-                j = js[jj]
-                dx = jnp.where(last_lane, turned_x[jj + 1], turned_x[jj]) - ux[jj]
-                dy = jnp.where(last_lane, turned_y[jj + 1], turned_y[jj]) - uy[jj]
-                ex = dx + 1.0
-                pull = (dx * (ex + 1.0) + dy * dy) * coef[0, j, at, :]
-                ax, ay = pull * ex, pull * dy
-                gx, gy = pltpu.roll(ax, 1, 1), pltpu.roll(ay, 1, 1)
-                fx = ax - jnp.where(first_lane, left_x, gx)
-                fy = ay - jnp.where(first_lane, left_y, gy)
-                left_x, left_y = gx, gy
-                hx, hy = down_pull(i, jj, ux[jj], uy[jj])
-                vx, vy = pltpu.roll(hx, 1, 0), pltpu.roll(hy, 1, 0)
-                fx = fx + (hx - jnp.where(first_sub, up_x[jj], vx))
-                fy = fy + (hy - jnp.where(first_sub, up_y[jj], vy))
-                up_x[jj], up_y[jj] = vx, vy
-                fx = fx + (tgt[sweep, 0, j, at, :] - hold * ux[jj])
-                fy = fy + (tgt[sweep, 1, j, at, :] - hold * uy[jj])
-                if damping is not None:
-                    fx = fx + damping * src[2, j, at, :]
-                    fy = fy + damping * src[3, j, at, :]
-                mobility = coef[2, j, at, :]
-                wx, wy = mobility * fx, mobility * fy
-                dst[0, j, at, :] = ux[jj] + wx
-                dst[1, j, at, :] = uy[jj] + wy
-                if final:
-                    dst[2, j, at, :] = wx * (1.0 / STEP_SIZE)
-                    dst[3, j, at, :] = wy * (1.0 / STEP_SIZE)
-                else:
-                    dst[2, j, at, :] = wx
-                    dst[3, j, at, :] = wy
-                if power and HALO // SUB <= i < nt - HALO // SUB:
-                    total = total + (wx * wx + wy * wy)
-            carry[k, 0, at, :] = left_x
-            carry[k, 1, at, :] = left_y
-        if power:
-            acc[...] += total
+                    tgt[sweep][n, j, pl.ds(HALO + SUB * i, SUB), :] = (below + above) * PULL
+
+    level, apply = substeps(rows, tiles_c, coef, carry, acc, hold)
 
     def reset():
-        for k in range(SUBSTEPS):
-            for n in range(2):
-                for i in range(nt):
-                    carry[k, n, pl.ds(SUB * i, SUB), :] = zero
+        clear_carry(carry, rows)
         acc[...] = zero
+
+    def forces(src, sweep):
+        def body(c, _):
+            level(0, c, src, pre, tgt[sweep], None, False, mode="pre")
+            return 0
+
+        reset()
+        lax.fori_loop(0, nc, body, 0)
 
     def chunk_in(c):
         return jnp.logical_and(c >= 0, c < nc)
@@ -354,7 +441,7 @@
 
     plain = DAMPING
 
-    def wave(w, order, sweep, first_damping, own_rows, final=False, power=True, before=None):
+    def wave(w, order, sweep, first_damping, own_rows, before=None, known=False):
         for k in range(SUBSTEPS):
             c = w - k
             last = k == SUBSTEPS - 1
@@ -363,11 +450,13 @@
             def _():
                 if before is not None and k == 1:
                     before(c)
-                level(
-                    k, c, order[k], order[k + 1], sweep,
-                    first_damping if k == 0 else plain,
-                    own_rows and last, power and last, final and last,
-                )
+                if known and k == 0:
+                    apply(c, order[0], pre, order[1], first_damping)
+                else:
+                    level(
+                        k, c, order[k], order[k + 1], tgt[sweep],
+                        first_damping if k == 0 else plain, own_rows and last, last,
+                    )
 
     def boundary(sweep, c):
         for d in range(2):
@@ -408,13 +497,12 @@
         return 0
 
     lax.fori_loop(0, nc + SUBSTEPS, round0, 0)
-    damping1 = spread_scale(0)
-
-    reset()
+    damping1 = spread_scale(0, lambda: forces(sa, 0))
+
     soon, ahead = min(3, nc), min(4, nc)
 
     def round1(w, _):
-        wave(w, (sa, sb, sa, sb, sc), 0, damping1, True)
+        wave(w, (sa, sb, sa, sb, sc), 0, damping1, True, known=True)
         c = w - (SUBSTEPS - 1)
 
         @pl.when(chunk_in(c))
@@ -465,34 +553,47 @@
         return 0
 
     lax.fori_loop(0, nc + SUBSTEPS, round2, 0)
-    damping3 = spread_scale(2)
-
-    reset()
-
-    def out_copies(j):
-        cols = pl.ds(pl.multiple_of(j * LANES, LANES), LANES)
-        return (
-            pltpu.make_async_copy(sa.at[0:2, j, own, :], out_u.at[:, 0, :, cols], out_sem.at[0]),
-            pltpu.make_async_copy(sa.at[2:4, j, own, :], out_v.at[:, 0, :, cols], out_sem.at[0]),
-        )
-
-    def round3(w, _):
-        wave(w, (sc, sb, sc, sb, sa), 1, damping3, True, final=True, power=False)
-        c = w - (SUBSTEPS - 1)
-
-        @pl.when(chunk_in(c))
-        def _():
-            for jj in range(WIDE):
-                for copy in out_copies(c * WIDE + jj):
-                    copy.start()
-
-        return 0
-
-    lax.fori_loop(0, nc + SUBSTEPS - 1, round3, 0)
-
+    damping_out[...] = spread_scale(2, lambda: forces(sc, 1))
     for sweep in range(2):
-        strip_wait_all(sends_to, tgt.at[sweep, :, :, top_halo, :], th_snd.at[sweep])
-    wait_bytes(sa.at[:, :, own, :], out_sem.at[0])
+        strip_wait_all(sends_to, tgt[sweep].at[:, :, top_halo, :], th_snd.at[sweep])
+
+
+def last_round(
+    ns, rows, tiles_c,
+    state, tgt, coef, pre, damping, out_u, out_v,
+    sa, sb, stage, carry, out_sem,
+):
+    nc = tiles_c // WIDE
+    level, apply = substeps(rows, tiles_c, coef, carry, None, pull_of(lax.axis_index("sec"), ns))
+    clear_carry(carry, rows)
+    first = damping[...]
+
+    def wave(w, _):
+        for k in range(SUBSTEPS):
+            c = w - k
+
+            @pl.when(jnp.logical_and(c >= 0, c < nc))
+            def _():
+                if k == 0:
+                    apply(c, state, pre, sb, first)
+                elif k == 1:
+                    level(k, c, sb, sa, tgt, DAMPING, False)
+                elif k == 2:
+                    level(k, c, sa, sb, tgt, DAMPING, False)
+                else:
+                    level(k, c, sb, stage, tgt, DAMPING, True, mode="final")
+                    for jj in range(WIDE):
+                        j = c * WIDE + jj
+                        cols = pl.ds(pl.multiple_of(j * LANES, LANES), LANES)
+                        for n, out in enumerate((out_u, out_v)):
+                            pltpu.make_async_copy(
+                                stage.at[n, :, j], out.at[:, 0, :, cols], out_sem.at[0]
+                            ).start()
+
+        return 0
+
+    lax.fori_loop(0, nc + SUBSTEPS - 1, wave, 0)
+    pltpu.make_async_copy(stage, stage, out_sem.at[0]).wait()
 
 
 def relax(mesh, start_offsets, section_flow, fixed_nodes, links_across, links_down):
@@ -502,23 +603,27 @@
     nc = tiles_c // WIDE
     padded = rows + 2 * HALO
     f32 = jnp.float32
-    state = pltpu.VMEM((4, tiles_c, padded + SUB, LANES), f32)
+    state = (4, tiles_c, padded + SUB, LANES)
+    planes = lambda n: (n, tiles_c, padded, LANES)
+    lines = pltpu.VMEM((SUBSTEPS, 2, padded, LANES), f32)
     dma = pltpu.SemaphoreType.DMA
-    out = jax.ShapeDtypeStruct(start_offsets.shape, f32)
-    return pl.pallas_call(
+    anywhere = pl.BlockSpec(memory_space=pltpu.HBM)
+    near = pl.BlockSpec(memory_space=pltpu.VMEM)
+    handed = (state, planes(2), planes(3), planes(2), (SUB, LANES))
+    between = pl.pallas_call(
         functools.partial(kernel, ns, nz, rows, tiles_c),
-        out_shape=(out, out),
-        in_specs=[pl.BlockSpec(memory_space=pl.ANY)] * 5,
-        out_specs=(pl.BlockSpec(memory_space=pl.ANY), pl.BlockSpec(memory_space=pl.ANY)),
+        out_shape=tuple(pltpu.VMEM(shape, f32) for shape in handed),
+        in_specs=[anywhere] * 5,
+        out_specs=(near,) * len(handed),
         scratch_shapes=[
-            state, state, state,
-            pltpu.VMEM((2, 2, tiles_c, padded, LANES), f32),
-            pltpu.VMEM((3, tiles_c, padded, LANES), f32),
-            pltpu.VMEM((3, tiles_c, padded, LANES), jnp.int32),
+            pltpu.VMEM(state, f32),
+            pltpu.VMEM(state, f32),
+            pltpu.VMEM(planes(2), f32),
+            pltpu.VMEM(planes(3), jnp.int32),
             pltpu.VMEM((2, tiles_c, rows, LANES), f32),
             pltpu.VMEM((2, 2, tiles_c, rows, LANES), f32),
             pltpu.VMEM((2, 2, 2, tiles_c, rows, LANES), f32),
-            pltpu.VMEM((SUBSTEPS, 2, padded, LANES), f32),
+            lines,
             pltpu.VMEM((SUB, LANES), f32),
             pltpu.VMEM((6, 1, LANES), f32),
             pltpu.VMEM((3, nz - 1, 1, LANES), f32),
@@ -529,12 +634,29 @@
             dma((2, 2)), dma((2, 2)),
             dma((2,)), dma((2,)),
             dma((3,)), dma((3,)), dma((3,)), dma((3,)),
+        ],
+        compiler_params=pltpu.CompilerParams(
+            collective_id=0, has_side_effects=True, vmem_limit_bytes=107 * 512 * 1024
+        ),
+    )(start_offsets, section_flow, fixed_nodes, links_across, links_down)
+    between = [pltpu.with_memory_space_constraint(x, pltpu.VMEM) for x in between]
+    out = jax.ShapeDtypeStruct(start_offsets.shape, f32)
+    return pl.pallas_call(
+        functools.partial(last_round, ns, rows, tiles_c),
+        out_shape=(out, out),
+        in_specs=[near] * len(handed),
+        out_specs=(anywhere, anywhere),
+        scratch_shapes=[
+            pltpu.VMEM(state, f32),
+            pltpu.VMEM(state, f32),
+            pltpu.VMEM((2, 2, tiles_c, rows, LANES), f32),
+            lines,
             dma((1,)),
         ],
         compiler_params=pltpu.CompilerParams(
-            collective_id=0, has_side_effects=True, vmem_limit_bytes=60 * 1024 * 1024
+            vmem_limit_bytes=24 * 1024 * 1024
         ),
-    )(start_offsets, section_flow, fixed_nodes, links_across, links_down)
+    )(*between)
 
 
 def solution(mesh):

time: 124 us -> 116 us (0.935)
  Pallas kernels: 120 us -> 115 us
  local copies, waits for them, and re-layouts: 3.97 us -> 0 us
    pallas_call x1, Pallas kernels: 120 us -> 105 us  [relax(): pl.pallas_call(functools.partial(kernel, ns, nz, rows, tiles_c), out_shap...]
    pallas_call x0 -> x1, Pallas kernels: none -> 10.5 us  [relax(): pl.pallas_call(functools.partial(last_round, ns, rows, tiles_c), out_shap...]
    unnamed x4 -> x0, local copies, waits for them, and re-layouts: 3.97 us -> none
where the time goes in v3:
time: 116 us
  Pallas kernels  115 us (99%)
    pallas_call x1, Pallas kernels, relax(): pl.pallas_call(functools.partial(kernel, ns, nz, rows, tiles_c), out_shap...  105 us
    pallas_call x1, Pallas kernels, relax(): pl.pallas_call(functools.partial(last_round, ns, rows, tiles_c), out_shap...  10.5 us

profile of v3, /device:TPU:1, one launch (start us, length us, event | category | flops | bytes accessed | tf_op | source)
XLA Modules:
  0.0 115.7 jit_solution(2826346839149712766)
XLA Ops:
  0.6 104.5 %shard_map.68 = (f32[4,16,120,128]{3,2,1,0:T(8,128)S(1)}, f32[2,16,112,128]{3,2,1,0:T(8,128)S(1)}, f32[3,16,112,128]{3,2,1,0:T(8,128)S(1)}, f32[2,16,112,128]{3,2,1,0:T(8,128)S(1)}, f32[8,128]{1,0:T(8,128)S(1)}) custom-call(f32[2,1,96,2048]{3,2,1,0:T(8,128)} %u0.1, f32[2,1,96,2048]{3,2,1,0:T(8,128)} %flow.1, s32[1,96,2048]{2,1,0:T(8,128)} %fixed.1, ...), custom_call_target="tpu_custom_call" | custom-call | tf_op jit(solution)/shard_map/pallas_call | solution.py:613
  105.2 10.5 %shard_map.69 = (f32[2,1,96,2048]{3,2,1,0:T(8,128)}, f32[2,1,96,2048]{3,2,1,0:T(8,128)}) custom-call(f32[4,16,120,128]{3,2,1,0:T(8,128)S(1)} %get-tuple-element.7.state, f32[2,16,112,128]{3,2,1,0:T(8,128)S(1)} %get-tuple-element.8.tgt, f32[3,16,112,128]{3,2,1,0:T(8,128)S(1)} %get-tuple-element.9.coef, f32[2,16,112,128]{3,2,1,0:T(8,128)S(1)} %get-tuple-element.10.pre, ...), custom_call_target="tpu_custom_call" | custom-call | tf_op jit(solution)/shard_map/pallas_call | solution.py:644

commit v4 on v3

--- a/solution.py
+++ b/solution.py
@@ -24,6 +24,10 @@
 WIDE = 2
 HALF = LANES // 2
 MESH = pl.DeviceIdType.MESH
+
+
+def wrap(x, n):
+    return jnp.where(x >= n, x - n, x)
 
 
 def vreg_iota(axis):
@@ -173,7 +177,7 @@
     nt = (rows + 2 * HALO) // SUB
     sec = lax.axis_index("sec")
     strip = lax.axis_index("strip")
-    sec_up, sec_dn = lax.rem(sec + 1, ns), lax.rem(sec + ns - 1, ns)
+    sec_up, sec_dn = wrap(sec + 1, ns), wrap(sec + ns - 1, ns)
     has_above_strip, has_below_strip = strip > 0, strip < nz - 1
     own = pl.ds(HALO, rows)
     tgt = (tgt0, tgt1)
@@ -181,11 +185,18 @@
     def wait_bytes(ref, sem):
         pltpu.make_async_copy(ref, ref, sem).wait()
 
-    def start_u(j, _):
-        cols = pl.ds(pl.multiple_of(j * LANES, LANES), LANES)
-        sem = ld_s.at[j // WIDE]
-        pltpu.make_async_copy(u0.at[:, 0, :, cols], sb.at[0:2, j, own, :], sem).start()
-        pltpu.make_async_copy(flow.at[:, 0, :, cols], sb.at[2:4, j, own, :], sem).start()
+    barrier = pltpu.get_barrier_semaphore()
+    for d in range(ns - 1, 0, -1):
+        pl.semaphore_signal(barrier, inc=1, device_id={"sec": wrap(sec + d, ns)}, device_id_type=MESH)
+    for d in range(nz - 1, 0, -1):
+        pl.semaphore_signal(barrier, inc=1, device_id={"strip": wrap(strip + d, nz)}, device_id_type=MESH)
+
+    def start_u(c, _):
+        for jj in range(WIDE):
+            j = c * WIDE + jj
+            cols = pl.ds(pl.multiple_of(j * LANES, LANES), LANES)
+            pltpu.make_async_copy(u0.at[:, 0, :, cols], sb.at[0:2, j, own, :], ld_s.at[c]).start()
+            pltpu.make_async_copy(flow.at[:, 0, :, cols], sb.at[2:4, j, own, :], ld_s.at[c]).start()
         return 0
 
     def start_g(j, _):
@@ -194,21 +205,7 @@
             pltpu.make_async_copy(ref.at[0, :, cols], raw.at[n, j, own, :], ld_g.at[0]).start()
         return 0
 
-    lax.fori_loop(0, tiles_c, start_u, 0)
-    lax.fori_loop(0, tiles_c, start_g, 0)
-
-    barrier = pltpu.get_barrier_semaphore()
-
-    def greet_strip(d, _):
-        pl.semaphore_signal(barrier, inc=1, device_id={"strip": lax.rem(strip + d, nz)}, device_id_type=MESH)
-        return 0
-
-    def greet_sec(d, _):
-        pl.semaphore_signal(barrier, inc=1, device_id={"sec": lax.rem(sec + d, ns)}, device_id_type=MESH)
-        return 0
-
-    lax.fori_loop(1, nz, greet_strip, 0)
-    lax.fori_loop(1, ns, greet_sec, 0)
+    lax.fori_loop(0, nc, start_u, 0)
 
     zero = jnp.zeros((SUB, LANES), jnp.float32)
     zero_i = jnp.zeros((SUB, LANES), jnp.int32)
@@ -343,6 +340,7 @@
     prepare(0)
     pl.semaphore_wait(barrier, nz - 1 + ns - 1)
     e_send(0, 0, sa)
+    lax.fori_loop(0, tiles_c, start_g, 0)
     lax.fori_loop(1, nc, first_sends, 0)
     strip_start(u_halo)
 
@@ -416,7 +414,7 @@
             pltpu.make_async_remote_copy(
                 src_ref=mine.at[2 * n], dst_ref=red1.at[n, d - 1],
                 send_sem=r1_snd.at[n], recv_sem=r1_rcv.at[n],
-                device_id={"strip": lax.rem(strip + d, nz)}, device_id_type=MESH,
+                device_id={"strip": wrap(strip + d, nz)}, device_id_type=MESH,
             ).start()
         if first_sent is not None:
             first_sent()
@@ -426,7 +424,7 @@
             pltpu.make_async_remote_copy(
                 src_ref=mine.at[2 * n + 1], dst_ref=red2.at[n, d - 1],
                 send_sem=r2_snd.at[n], recv_sem=r2_rcv.at[n],
-                device_id={"sec": lax.rem(sec + d, ns)}, device_id_type=MESH,
+                device_id={"sec": wrap(sec + d, ns)}, device_id_type=MESH,
             ).start()
         if second_sent is not None:
             second_sent()

time: 116 us -> 115 us (level)
  no operation moved by 1% of the time
where the time goes in v4:
time: 115 us
  Pallas kernels  114 us (99%)
    pallas_call x1, Pallas kernels, relax(): pl.pallas_call(functools.partial(kernel, ns, nz, rows, tiles_c), out_shap...  104 us
    pallas_call x1, Pallas kernels, relax(): pl.pallas_call(functools.partial(last_round, ns, rows, tiles_c), out_shap...  10.5 us

profile of v4, /device:TPU:1, one launch (start us, length us, event | category | flops | bytes accessed | tf_op | source)
XLA Modules:
  0.0 115.1 jit_solution(2024325525825938345)
XLA Ops:
  0.6 103.9 %shard_map.68 = (f32[4,16,120,128]{3,2,1,0:T(8,128)S(1)}, f32[2,16,112,128]{3,2,1,0:T(8,128)S(1)}, f32[3,16,112,128]{3,2,1,0:T(8,128)S(1)}, f32[2,16,112,128]{3,2,1,0:T(8,128)S(1)}, f32[8,128]{1,0:T(8,128)S(1)}) custom-call(f32[2,1,96,2048]{3,2,1,0:T(8,128)} %u0.1, f32[2,1,96,2048]{3,2,1,0:T(8,128)} %flow.1, s32[1,96,2048]{2,1,0:T(8,128)} %fixed.1, ...), custom_call_target="tpu_custom_call" | custom-call | tf_op jit(solution)/shard_map/pallas_call | solution.py:611
  104.6 10.5 %shard_map.69 = (f32[2,1,96,2048]{3,2,1,0:T(8,128)}, f32[2,1,96,2048]{3,2,1,0:T(8,128)}) custom-call(f32[4,16,120,128]{3,2,1,0:T(8,128)S(1)} %get-tuple-element.7.state, f32[2,16,112,128]{3,2,1,0:T(8,128)S(1)} %get-tuple-element.8.tgt, f32[3,16,112,128]{3,2,1,0:T(8,128)S(1)} %get-tuple-element.9.coef, f32[2,16,112,128]{3,2,1,0:T(8,128)S(1)} %get-tuple-element.10.pre, ...), custom_call_target="tpu_custom_call" | custom-call | tf_op jit(solution)/shard_map/pallas_call | solution.py:642
